TPU v7x, 32 devices: a whole 2x2x4 slice. The times are simulated.
32 devices in a mesh: round: 2 (over x), seq: 16 (over z, y, core).
Axes of the slice: x: 2, y: 2, z: 4, core: 2. Of those that a mesh axis runs over, the one named last changes fastest.
Arguments:
- qk: bfloat16 [8192, 1024], P('seq'), may hold values from -96 to 96
- values: bfloat16 [8192, 1024], P('seq'), may hold values from -6 to 6
- dest_dev: int32 [2, 8192], P('round', 'seq'), may hold values from 0 to 15, as said below
- dest_slot: int32 [2, 8192], P('round', 'seq'), may hold values from 0 to 511, as said below
Outputs:
- merged: bfloat16 [8192, 1024], P('seq', 'round')
Inputs may be any that keep to these rules, and one draw needn't show every extreme that they name: dest_dev and dest_slot together send each round's 8192 tokens to 8192 distinct positions. In each round, from the rows of one index of seq at most 48 go to any one index of seq, and exactly 48 for some pair; every index receives exactly 512 rows. `dest_slot`: the row within the destination's block, see dest_dev.
All inputs are finite; a program needn't handle non-finite values.
Results may differ from a plain program's by a relative error of at most 0.03.
Values may be sent and summed in bfloat16 or wider, within the bound.
A program may use at most 64 MiB of HBM per device.

v0:
```python
import jax
import jax.numpy as jnp
from jax import lax
from jax.experimental import pallas as pl
from jax.experimental.pallas import tpu as pltpu
from jax.sharding import PartitionSpec as P

HEAD_DIM = 128
STRETCH = 512


eps_norm = 1e-06
self_score = -100000.0


def passed_along(value, axis, steps):
    count = lax.axis_size(axis)
    pairs = [(source, (source + steps) % count) for source in range(count)]
    return lax.ppermute(value, axis, pairs)


def as_sent(array):
    return jax.tree.map(lambda a: a.astype(jnp.bfloat16) if a.dtype == jnp.float32 else a, array)


def unit_keys(rows):
    count = rows.shape[0]
    heads = rows.shape[1] // HEAD_DIM
    field = rows.astype(jnp.float32).reshape(count, heads, HEAD_DIM)
    field = field * lax.rsqrt(jnp.sum(field * field, axis=-1, keepdims=True) + eps_norm)
    return field.reshape(count, heads * HEAD_DIM).astype(jnp.bfloat16)


def spread_heads(weights):
    return jnp.repeat(weights, HEAD_DIM, axis=1)


def pack_round(qk, values, dest, slot, shards, cap):
    rows = qk.shape[0]
    hits = (dest[:, None] == jnp.arange(shards, dtype=jnp.int32)[None, :]).astype(jnp.int32)
    ranks = jnp.sum(hits * jnp.cumsum(hits, axis=0), axis=1) - 1
    position = dest * cap + ranks
    total = shards * cap
    send_qk = jnp.zeros((total, qk.shape[1]), qk.dtype).at[position].set(qk)
    send_values = jnp.zeros((total, values.shape[1]), values.dtype).at[position].set(values)
    send_slot = jnp.full((total,), rows, jnp.int32).at[position].set(slot)
    send_source = (
        jnp.full((total,), rows, jnp.int32).at[position].set(jnp.arange(rows, dtype=jnp.int32))
    )
    return (send_qk, send_values, send_slot, send_source)


def group_attend(queries, keys, vals):
    rows = queries.shape[0]
    heads = queries.shape[1] // HEAD_DIM
    qpart = queries.reshape(rows, heads, HEAD_DIM)
    kpart = keys.reshape(2 * rows, heads, HEAD_DIM)
    vpart = vals.reshape(2 * rows, heads, HEAD_DIM)
    scores = jnp.einsum("qhd,khd->hqk", qpart, kpart, preferred_element_type=jnp.float32)
    itself = (
        jnp.arange(2 * rows, dtype=jnp.int32)[None, :]
        == jnp.arange(rows, dtype=jnp.int32)[:, None] + rows
    )
    scores = jnp.where(itself[None], jnp.float32(self_score), scores)
    highest = jnp.max(scores, axis=-1)
    lse = highest + jnp.log(jnp.sum(jnp.exp(scores - highest[..., None]), axis=-1))
    probs = jnp.exp(scores - lse[..., None]).astype(jnp.bfloat16)
    attended = jnp.einsum("hqk,khd->qhd", probs, vpart, preferred_element_type=jnp.float32)
    return (attended.reshape(rows, heads * HEAD_DIM).astype(jnp.bfloat16), jnp.transpose(lse))


def attend_sorted(sorted_qk, sorted_values):
    rows = sorted_qk.shape[0]
    width = sorted_qk.shape[1]
    keys = unit_keys(sorted_qk)
    before_keys, before_values = passed_along((keys, sorted_values), "seq", 1)
    ext_keys = jnp.concatenate([before_keys, keys], axis=0)
    ext_values = jnp.concatenate([before_values, sorted_values], axis=0)
    group_width = width // 2

    def one_stretch(position):
        pieces = []
        totals = []
        for group in range(2):
            low = group * group_width
            high = low + group_width
            piece, total = group_attend(
                sorted_qk[:, low:high], ext_keys[:, low:high], ext_values[:, low:high]
            )
            pieces.append(piece)
            totals.append(total)
        return (jnp.concatenate(pieces, axis=1), jnp.concatenate(totals, axis=1))

    attended, lse = lax.map(one_stretch, jnp.arange(rows // STRETCH, dtype=jnp.int32))
    return (attended.reshape(rows, width), lse.reshape(rows, lse.shape[-1]))


def on_device(qk, values, dest_dev, dest_slot):
    shards = lax.axis_size("seq")
    rows = qk.shape[0]
    width = qk.shape[1]
    heads = width // HEAD_DIM
    cap = 3 * (rows // (2 * shards))
    send_qk, send_values, send_slot, send_source = pack_round(
        qk, values, dest_dev[0], dest_slot[0], shards, cap
    )
    got_qk, got_values, got_slot, got_source = (
        lax.all_to_all(send_qk, "seq", split_axis=0, concat_axis=0, tiled=True),
        lax.all_to_all(send_values, "seq", split_axis=0, concat_axis=0, tiled=True),
        lax.all_to_all(send_slot, "seq", split_axis=0, concat_axis=0, tiled=True),
        lax.all_to_all(send_source, "seq", split_axis=0, concat_axis=0, tiled=True),
    )
    sorted_qk = jnp.zeros((rows, width), jnp.bfloat16).at[got_slot].set(got_qk, mode="drop")
    sorted_values = jnp.zeros((rows, width), jnp.bfloat16).at[got_slot].set(got_values, mode="drop")
    attended, lse = attend_sorted(sorted_qk, sorted_values)
    lse = lse.reshape(rows, heads)
    picked = jnp.clip(got_slot, 0, rows - 1)
    reply_out = attended[picked]
    reply_lse = lse[picked]
    back_out, back_lse, back_ids = (
        lax.all_to_all(as_sent(reply_out), "seq", split_axis=0, concat_axis=0, tiled=True).astype(
            reply_out.dtype
        ),
        lax.all_to_all(as_sent(reply_lse), "seq", split_axis=0, concat_axis=0, tiled=True).astype(
            reply_lse.dtype
        ),
        lax.all_to_all(got_source, "seq", split_axis=0, concat_axis=0, tiled=True),
    )
    round_out = jnp.zeros((rows, width), jnp.bfloat16).at[back_ids].set(back_out, mode="drop")
    round_lse = jnp.zeros((rows, heads), jnp.float32).at[back_ids].set(back_lse, mode="drop")
    local_top = round_lse
    local_top = lax.pmax(local_top, "round")
    denom = jnp.exp(round_lse - local_top)
    numer = spread_heads(denom) * round_out.astype(jnp.float32)
    numer_half, denom_half = (
        lax.psum_scatter(
            numer.astype(jnp.bfloat16), "round", scatter_dimension=1, tiled=True
        ).astype(jnp.float32),
        lax.psum_scatter(
            denom.astype(jnp.bfloat16), "round", scatter_dimension=1, tiled=True
        ).astype(jnp.float32),
    )
    merged = numer_half / spread_heads(denom_half)
    return merged.astype(jnp.bfloat16)


NO_ROW = -1e30
CHUNK = 16


def by_head(array, side, heads):
    wide = heads * HEAD_DIM
    part = lax.dynamic_slice_in_dim(array, side * wide, wide, 1)
    return jnp.transpose(part.reshape(array.shape[0], heads, HEAD_DIM), (1, 0, 2))


def local_kernel(
    put_ref, take_ref, tokens_ref, out_ref, lse_ref, wide_q, wide_v, sorted_q, sorted_v, att, logs
):
    blocks, _, rows, _ = tokens_ref.shape
    bound = sorted_q.shape[0] - 8

    @pl.loop(0, blocks)
    def _(block):
        wide_q[...] = tokens_ref[block, 0].astype(jnp.float32)
        wide_v[...] = tokens_ref[block, 1].astype(jnp.float32)

        @pl.loop(0, rows, step=CHUNK)
        def _(start):
            for row in range(CHUNK):
                to = put_ref[block * rows + start + row]
                sorted_q[pl.ds(to, 1), :] = wide_q[pl.ds(start + row, 1), :]
                sorted_v[pl.ds(to, 1), :] = wide_v[pl.ds(start + row, 1), :]

    att[pl.ds(bound, 8), :] = jnp.zeros((8, HEAD_DIM), jnp.float32)
    logs[pl.ds(bound, 8), :] = jnp.full((8, HEAD_DIM), NO_ROW, jnp.float32)

    @pl.loop(0, bound // STRETCH - 1)
    def _(stretch):
        low = pl.multiple_of(stretch * STRETCH, STRETCH)
        own = pl.multiple_of(low + STRETCH, STRETCH)
        queries = sorted_q[pl.ds(own, STRETCH), :].astype(jnp.bfloat16)
        field = sorted_q[pl.ds(low, 2 * STRETCH), :]
        scale = lax.rsqrt(jnp.sum(field * field, axis=-1, keepdims=True) + eps_norm)
        keys = (field * scale).astype(jnp.bfloat16)
        vals = sorted_v[pl.ds(low, 2 * STRETCH), :].astype(jnp.bfloat16)
        scores = lax.dot_general(
            queries, keys, (((1,), (1,)), ((), ())), preferred_element_type=jnp.float32
        )
        row_at = lax.broadcasted_iota(jnp.int32, scores.shape, 0) + STRETCH
        col_at = lax.broadcasted_iota(jnp.int32, scores.shape, 1)
        scores = jnp.where(row_at == col_at, jnp.float32(self_score), scores)
        highest = jnp.max(scores, axis=-1, keepdims=True)
        probs = jnp.exp(scores - highest)
        weight = jnp.sum(probs, axis=-1, keepdims=True)
        attended = jnp.dot(probs.astype(jnp.bfloat16), vals, preferred_element_type=jnp.float32)
        att[pl.ds(own, STRETCH), :] = attended / weight
        logs[pl.ds(own, STRETCH), :] = jnp.broadcast_to(
            highest + jnp.log(weight), (STRETCH, HEAD_DIM)
        )

    @pl.loop(0, blocks)
    def _(block):
        @pl.loop(0, rows, step=CHUNK)
        def _(start):
            for row in range(CHUNK):
                at = take_ref[block * rows + start + row]
                wide_q[pl.ds(start + row, 1), :] = att[pl.ds(at, 1), :]
                wide_v[pl.ds(start + row, 1), :] = logs[pl.ds(at, 1), :]

        out_ref[block] = wide_q[...].astype(jnp.bfloat16)
        lse_ref[block] = jnp.transpose(wide_v[...])[0:1, :]


def local_attend(put, take, tokens, section):
    blocks, _, rows, wide = tokens.shape
    bound = section + STRETCH + 8
    return pl.pallas_call(
        local_kernel,
        out_shape=(
            jax.ShapeDtypeStruct((blocks, rows, wide), jnp.bfloat16),
            jax.ShapeDtypeStruct((blocks, 1, rows), jnp.float32),
        ),
        in_specs=[
            pl.BlockSpec(memory_space=pltpu.SMEM),
            pl.BlockSpec(memory_space=pltpu.SMEM),
            pl.BlockSpec(memory_space=pltpu.VMEM),
        ],
        out_specs=(
            pl.BlockSpec(memory_space=pltpu.VMEM),
            pl.BlockSpec(memory_space=pltpu.VMEM),
        ),
        scratch_shapes=[
            pltpu.VMEM((rows, wide), jnp.float32),
            pltpu.VMEM((rows, wide), jnp.float32),
            pltpu.VMEM((bound, wide), jnp.float32),
            pltpu.VMEM((bound, wide), jnp.float32),
            pltpu.VMEM((bound, wide), jnp.float32),
            pltpu.VMEM((bound, wide), jnp.float32),
        ],
        compiler_params=pltpu.CompilerParams(vmem_limit_bytes=48 * 1024 * 1024),
        name="local_attend",
    )(put, take, tokens)


def head_groups(shards, heads):
    group = shards // heads
    along = [[lane + group * step for step in range(heads)] for lane in range(group)]
    within = [[group * step + lane for lane in range(group)] for step in range(heads)]
    return group, along, within


def slots_of(place, section, base, total):
    bound = section + STRETCH
    put = jnp.minimum(lax.rem(place - base + STRETCH + total, total), bound)
    take = jnp.where(put < STRETCH, bound, put)
    return put, take


def by_heads_on_device(qk, values, dest_dev, dest_slot):
    shards = lax.axis_size("seq")
    sides = lax.axis_size("round")
    rows, width = qk.shape
    heads = width // HEAD_DIM // sides
    total = rows * shards
    group, along, within = head_groups(shards, heads)
    parts = group // sides
    section = total // parts
    side = lax.axis_index("round")
    lane = lax.rem(lax.axis_index("seq"), group)
    place = dest_dev[0] * rows + dest_slot[0]
    places = lax.all_gather(place, ("round", "seq")).reshape(sides, shards, rows)
    mine = lax.dynamic_index_in_dim(places, lane // parts, 0, keepdims=False)
    mine = jnp.transpose(mine.reshape(heads, group, rows), (1, 0, 2)).reshape(-1)
    put, take = slots_of(mine, section, lax.rem(lane, parts) * section, total)
    packed = jnp.stack([by_head(qk, side, heads), by_head(values, side, heads)], axis=1)
    packed = lax.all_to_all(
        packed, "seq", split_axis=0, concat_axis=0, tiled=True, axis_index_groups=along
    )
    tokens = lax.all_gather(packed, "seq", axis_index_groups=within)
    tokens = tokens.reshape(shards, 2, rows, HEAD_DIM)
    out, lse = local_attend(put, take, tokens, section)
    out = lax.all_to_all(
        out, "seq", split_axis=0, concat_axis=0, tiled=True, axis_index_groups=within
    ).reshape(group, heads, rows, HEAD_DIM)
    lse = lax.all_to_all(
        lse, "seq", split_axis=0, concat_axis=0, tiled=True, axis_index_groups=within
    ).reshape(group, heads, rows)
    weight = jnp.exp(lse - jnp.max(lse, axis=0, keepdims=True))
    weight = weight / jnp.sum(weight, axis=0, keepdims=True)
    merged = jnp.sum(weight[..., None] * out.astype(jnp.float32), axis=0).astype(jnp.bfloat16)
    merged = lax.all_to_all(
        merged, "seq", split_axis=0, concat_axis=0, tiled=True, axis_index_groups=along
    )
    return jnp.transpose(merged, (1, 0, 2)).reshape(rows, heads * HEAD_DIM)


def whole_head_fits(qk, shards, sides):
    rows, width = qk.shape
    heads = width // HEAD_DIM // sides
    bytes_held = rows * HEAD_DIM * shards * 2 * 2
    if shards % heads or (shards // heads) % sides:
        return False
    parts = shards // heads // sides
    if (rows * shards) % (parts * STRETCH) or parts < 2:
        return False
    return bytes_held <= 8 * 1024 * 1024


def either_plan(qk, values, dest_dev, dest_slot):
    if whole_head_fits(qk, lax.axis_size("seq"), lax.axis_size("round")):
        return by_heads_on_device(qk, values, dest_dev, dest_slot)
    return on_device(qk, values, dest_dev, dest_slot)


def solution(mesh):
    return jax.shard_map(
        either_plan,
        mesh=mesh,
        in_specs=(P("seq", None), P("seq", None), P("round", "seq"), P("round", "seq")),
        out_specs=P("seq", "round"),
        check_vma=False,
    )
```

profile of v0, /device:TPU:0, one launch (start us, length us, event | category | flops | bytes accessed | tf_op | source)
XLA Modules:
  0.0 185.3 jit_solution(15067746746459166016)
XLA Ops:
  6.5 0.0 all-gather.4.cloned.1.call-start
  6.5 1.3 constant_dynamic-slice_fusion
  7.8 0.2 copy.34
  8.0 0.2 copy.33
  8.2 0.1 pad_maximum_fusion
  8.3 0.0 copy-start
  8.4 0.0 copy-start.1
  8.4 0.1 copy.27
  8.4 31.9 %all_to_all.20 = bf16[4,2,512,128]{2,3,1,0:T(8,128)(2,1)S(1)} all-to-all(bf16[4,2,512,128]{2,3,1,0:T(8,128)(2,1)S(1)} %copy.27), channel_id=1, replica_groups={{0,4,8,12},{1,5,9,13},{2,6,10,14},{3,7,11,15},{16,20,24,28},{17,21,25,2..., dimensions={0} | all-to-all | bytes 2097152 | tf_op jit(solution)/shard_map/all_to_all | solution.py:277
  40.3 1.3 copy.28
  41.6 0.0 all-gather.4.cloned.1.call-update
  41.7 0.0 copy-done
  41.7 0.0 copy-done.1
  41.7 40.3 %all-gather.1 = s32[32,1,512]{2,1,0:T(1,128)S(1)} all-gather(s32[1,1,512]{2,1,0:T(1,128)S(1)} %add_bitcast_fusion), channel_id=1, replica_groups=mesh['round'=2,'seq'=16] {'round','seq'}, dimensions={0}, use_global_device_ids=true | all-gather | bytes 67584 | tf_op jit(solution)/shard_map/all_gather | solution.py:272
  82.2 0.0 all-gather.4.cloned.1.call-done.tokens_ref
  82.2 41.3 %local_attend.1 = (bf16[16,512,128]{2,1,0:T(8,128)(2,1)}, f32[16,1,512]{2,1,0:T(1,128)S(1)}) custom-call(s32[8192]{0:T(1024)S(1)} %get-tuple-element.10.put_ref, s32[8192]{0:T(1024)S(1)} %get-tuple-element.9.take_ref, bf16[16,2,512,128]{3,2,1,0:T(8,128)(2,1)} %all-gather.4.cloned.1.call-done.tokens_ref), custom_call_target="tpu_custom_call" | custom-call | tf_op jit(solution)/shard_map/local_attend/pallas_call | solution.py:218
  123.5 6.3 %all_to_all.21 = f32[16,1,512]{2,1,0:T(1,128)S(1)} all-to-all(f32[16,1,512]{2,1,0:T(1,128)S(1)} %get-tuple-element.7), channel_id=1, replica_groups={{0,1,2,3},{4,5,6,7},{8,9,10,11},{12,13,14,15},{16,17,18,19},{20,21,22,2..., dimensions={0} | all-to-all | bytes 65536 | tf_op jit(solution)/shard_map/all_to_all | solution.py:286
  129.8 3.6 %all-to-all-start.2 = ((bf16[16,512,128]{2,1,0:T(8,128)(2,1)}), bf16[16,512,128]{2,1,0:T(8,128)(2,1)S(1)}, u32[]{:S(2)}, u32[]{:S(2)}) async-start(bf16[16,512,128]{2,1,0:T(8,128)(2,1)} %get-tuple-element.8), calls=%async_computation.2 | async-start | bytes 4194304 | tf_op jit(solution)/shard_map/all_to_all | solution.py:283
  133.4 0.1 reduce
  133.6 25.4 %all-to-all-done.2 = bf16[16,512,128]{2,1,0:T(8,128)(2,1)S(1)} async-done(((bf16[16,512,128]{2,1,0:T(8,128)(2,1)}), bf16[16,512,128]{2,1,0:T(8,128)(2,1)S(1)}, u32[]{:S(2)}, u32[]{:S(2)}) %all-to-all-start.2) | async-done | bytes 2097184 | tf_op jit(solution)/shard_map/all_to_all | solution.py:283
  159.0 1.4 fusion
  160.4 16.9 %all_to_all.22 = bf16[4,512,128]{2,1,0:T(8,128)(2,1)S(1)} all-to-all(bf16[4,512,128]{2,1,0:T(8,128)(2,1)S(1)} %fusion), channel_id=1, replica_groups={{0,4,8,12},{1,5,9,13},{2,6,10,14},{3,7,11,15},{16,20,24,28},{17,21,25,2..., dimensions={0} | all-to-all | bytes 1048576 | tf_op jit(solution)/shard_map/all_to_all | solution.py:292
  177.3 0.2 copy.29
  177.5 1.0 copy.30
  (13 shorter events, 0.2 us)
Async XLA Ops:
  6.5 75.6 %all-gather.4.cloned.1.call-start = ((), (), s32[]{:S(2)}) async-start(), calls=%async_computation.4 | async-start | bytes 5242880 | tf_op jit(solution)/shard_map/all_gather | solution.py:280
  8.3 33.4 %copy-start = (s32[1,512]{1,0:T(1,128)S(1)}, s32[1,512]{1,0:T(1,128)}, u32[]{:S(2)}) copy-start(s32[1,512]{1,0:T(1,128)} %param.7) | copy-start | bytes 6148
  8.4 33.4 %copy-start.1 = (s32[1,512]{1,0:T(1,128)S(1)}, s32[1,512]{1,0:T(1,128)}, u32[]{:S(2)}) copy-start(s32[1,512]{1,0:T(1,128)} %param.6) | copy-start | bytes 6148
  129.8 29.2 %all-to-all-start.2 = ((bf16[16,512,128]{2,1,0:T(8,128)(2,1)}), bf16[16,512,128]{2,1,0:T(8,128)(2,1)S(1)}, u32[]{:S(2)}, u32[]{:S(2)}) async-start(bf16[16,512,128]{2,1,0:T(8,128)(2,1)} %get-tuple-element.8), calls=%async_computation.2 | async-start | bytes 4194304 | tf_op jit(solution)/shard_map/all_to_all | solution.py:283
Sparse Core Ops, SparseCore 0:
  41.8 34.0 all-gather.3
where the time goes:
time: 186 us; the launch traced here: 185 us
  blocking collectives  95.4 us (51%)
  Pallas kernels  41.3 us (22%)
  waiting for transfers between devices  25.5 us (14%)
  between operations  13.6 us (7%)
  local copies, waits for them, and re-layouts  4.39 us (2%)
  starting transfers between devices  3.61 us (2%)
    pallas_call x1, Pallas kernels, local_attend(): pl.pallas_call(local_kernel, out_shape=(jax.ShapeDtypeStruct((blocks, row...  41.3 us
    all_gather x1, blocking collectives, by_heads_on_device(): lax.all_gather(place, ('round', 'seq')).reshape(sides, shards, rows)  40.3 us
    all_to_all x1, blocking collectives, by_heads_on_device(): lax.all_to_all(packed, 'seq', split_axis=0, concat_axis=0, tiled=True, ax...  31.9 us
    all_to_all x1, waiting for transfers between devices, by_heads_on_device(): lax.all_to_all(out, 'seq', split_axis=0, concat_axis=0, tiled=True, axis_...  25.4 us
    all_to_all x1, blocking collectives, by_heads_on_device(): lax.all_to_all(merged, 'seq', split_axis=0, concat_axis=0, tiled=True, ax...  16.9 us
    all_to_all x1, blocking collectives, by_heads_on_device(): lax.all_to_all(lse, 'seq', split_axis=0, concat_axis=0, tiled=True, axis_...  6.29 us
  transfers between devices with their start and end apart: 2, of which 1 were waited for; matrix products, arithmetic and copies ran while one was open for 0% of the time, Pallas kernels for 0%

commit v1 on v0

--- a/solution.py
+++ b/solution.py
@@ -1,3 +1,5 @@
+import functools
+
 import jax
 import jax.numpy as jnp
 from jax import lax
@@ -146,12 +148,6 @@
 
 NO_ROW = -1e30
 CHUNK = 16
-
-
-def by_head(array, side, heads):
-    wide = heads * HEAD_DIM
-    part = lax.dynamic_slice_in_dim(array, side * wide, wide, 1)
-    return jnp.transpose(part.reshape(array.shape[0], heads, HEAD_DIM), (1, 0, 2))
 
 
 def local_kernel(
@@ -243,6 +239,192 @@
     )(put, take, tokens)
 
 
+MESH = pl.DeviceIdType.MESH
+
+
+def near_first(count):
+    return sorted(range(1, count), key=lambda step: min(step, count - step))
+
+
+def greet_all(sides, shards, side, seat):
+    barrier = pltpu.get_barrier_semaphore()
+    for across in range(sides):
+        for step in range(shards):
+            if across or step:
+                pl.semaphore_signal(
+                    barrier,
+                    inc=1,
+                    device_id=(lax.rem(side + across, sides), lax.rem(seat + step, shards)),
+                    device_id_type=MESH,
+                )
+    pl.semaphore_wait(barrier, sides * shards - 1)
+
+
+def bring_kernel(
+    plan, qk_ref, values_ref, place_ref, tokens_ref, places_ref,
+    own_sem, line_send, line_recv, far_send, far_recv, near_send, near_recv, put_send, put_recv,
+):
+    sides, shards, heads, fars, nears = plan
+    group = fars * nears
+    side, seat = lax.axis_index("round"), lax.axis_index("seq")
+    level, lane = seat // group, lax.rem(seat, group)
+    far, near = lane // nears, lax.rem(lane, nears)
+
+    def columns(head):
+        return pl.ds(pl.multiple_of((side * heads + head) * HEAD_DIM, HEAD_DIM), HEAD_DIM)
+
+    def seat_of(level, far, near):
+        return level * group + far * nears + near
+
+    def block_of(level, far, near):
+        return (far * nears + near) * heads + level
+
+    def remote(source, target, send, recv, to):
+        return pltpu.make_async_remote_copy(
+            src_ref=source, dst_ref=target, send_sem=send, recv_sem=recv,
+            device_id=(side, to), device_id_type=MESH,
+        )
+
+    fields = (qk_ref, values_ref)
+    mine = block_of(level, far, near)
+    own = [
+        pltpu.make_async_copy(fields[k].at[:, columns(level)], tokens_ref.at[mine, k], own_sem.at[k])
+        for k in range(2)
+    ]
+    for copy in own:
+        copy.start()
+    greet_all(sides, shards, side, seat)
+
+    sent = []
+    line = {}
+    for k in range(2):
+        for step in near_first(heads):
+            to = lax.rem(level + step, heads)
+            copy = remote(
+                fields[k].at[:, columns(to)], tokens_ref.at[mine, k],
+                line_send.at[step - 1, k], line_recv.at[step - 1, k], seat_of(to, far, near),
+            )
+            copy.start()
+            sent.append(copy)
+            line[step, k] = copy
+
+    puts = []
+    for across in range(sides):
+        for step in range(heads):
+            for turn in range(nears):
+                at = (across * heads + step) * nears + turn
+                to = seat_of(lax.rem(level + step, heads), side, lax.rem(near + turn, nears))
+                copy = pltpu.make_async_remote_copy(
+                    src_ref=place_ref, dst_ref=places_ref.at[mine],
+                    send_sem=put_send.at[at], recv_sem=put_recv.at[mine],
+                    device_id=(lax.rem(side + across, sides), to), device_id_type=MESH,
+                )
+                puts.append(copy)
+                if at:
+                    copy.start()
+    stays = pltpu.make_async_copy(place_ref, places_ref.at[mine], put_recv.at[mine])
+    pl.when(far != side)(puts[0].start)
+    pl.when(far == side)(stays.start)
+
+    def pass_near(block, k, index):
+        for turn in range(1, nears):
+            copy = remote(
+                tokens_ref.at[block, k], tokens_ref.at[block, k],
+                near_send.at[turn - 1, index, k], near_recv.at[turn - 1, index, k],
+                seat_of(level, far, lax.rem(near + turn, nears)),
+            )
+            copy.start()
+            sent.append(copy)
+
+    def pass_far(block, k, step):
+        for turn in range(1, fars):
+            copy = remote(
+                tokens_ref.at[block, k], tokens_ref.at[block, k],
+                far_send.at[turn - 1, step, k], far_recv.at[turn - 1, step, k],
+                seat_of(level, lax.rem(far + turn, fars), near),
+            )
+            copy.start()
+            sent.append(copy)
+
+    def from_far(k, step):
+        for turn in range(1, fars):
+            source = block_of(
+                lax.rem(level + heads - step, heads), lax.rem(far + fars - turn, fars), near
+            )
+            remote(
+                tokens_ref.at[source, k], tokens_ref.at[source, k],
+                far_send.at[turn - 1, step, k], far_recv.at[turn - 1, step, k], seat,
+            ).wait_recv()
+            pass_near(source, k, turn * heads + step)
+
+    order = [(step, k) for k in range(2) for step in near_first(heads)]
+    for k in range(2):
+        own[k].wait()
+        pass_far(mine, k, 0)
+        pass_near(mine, k, 0)
+    late = [(0, 0), (0, 1)]
+    for step, k in order:
+        source = block_of(lax.rem(level + heads - step, heads), far, near)
+        line[step, k].wait_recv()
+        pass_far(source, k, step)
+        pass_near(source, k, step)
+        from_far(late[0][1], late[0][0])
+        late = late[1:] + [(step, k)]
+    for step, k in late:
+        from_far(k, step)
+    for turn in range(1, nears):
+        for away in range(fars):
+            for step in range(heads):
+                for k in range(2):
+                    source = block_of(
+                        lax.rem(level + heads - step, heads),
+                        lax.rem(far + fars - away, fars),
+                        lax.rem(near + nears - turn, nears),
+                    )
+                    index = away * heads + step
+                    remote(
+                        tokens_ref.at[source, k], tokens_ref.at[source, k],
+                        near_send.at[turn - 1, index, k], near_recv.at[turn - 1, index, k], seat,
+                    ).wait_recv()
+    for block in range(shards):
+        pltpu.make_async_copy(place_ref, places_ref.at[block], put_recv.at[block]).wait()
+    for copy in sent:
+        copy.wait_send()
+    for copy in puts[1:]:
+        copy.wait_send()
+    pl.when(far != side)(puts[0].wait_send)
+
+
+def bring_in(qk, values, place, plan):
+    sides, shards, heads, fars, nears = plan
+    rows = qk.shape[0]
+    dma = pltpu.SemaphoreType.DMA
+    return pl.pallas_call(
+        functools.partial(bring_kernel, plan),
+        out_shape=(
+            jax.ShapeDtypeStruct((shards, 2, rows, HEAD_DIM), jnp.bfloat16),
+            jax.ShapeDtypeStruct((shards,) + place.shape, jnp.int32),
+        ),
+        in_specs=[pl.BlockSpec(memory_space=pltpu.VMEM)] * 3,
+        out_specs=(pl.BlockSpec(memory_space=pl.ANY), pl.BlockSpec(memory_space=pl.ANY)),
+        scratch_shapes=[
+            dma((2,)),
+            dma((heads - 1, 2)),
+            dma((heads - 1, 2)),
+            dma((fars - 1, heads, 2)),
+            dma((fars - 1, heads, 2)),
+            dma((nears - 1, fars * heads, 2)),
+            dma((nears - 1, fars * heads, 2)),
+            dma((sides * heads * nears,)),
+            dma((shards,)),
+        ],
+        compiler_params=pltpu.CompilerParams(
+            collective_id=0, has_side_effects=True, vmem_limit_bytes=16 * 1024 * 1024
+        ),
+        name="bring_in",
+    )(qk, values, place)
+
+
 def head_groups(shards, heads):
     group = shards // heads
     along = [[lane + group * step for step in range(heads)] for lane in range(group)]
@@ -266,19 +448,11 @@
     group, along, within = head_groups(shards, heads)
     parts = group // sides
     section = total // parts
-    side = lax.axis_index("round")
     lane = lax.rem(lax.axis_index("seq"), group)
     place = dest_dev[0] * rows + dest_slot[0]
-    places = lax.all_gather(place, ("round", "seq")).reshape(sides, shards, rows)
-    mine = lax.dynamic_index_in_dim(places, lane // parts, 0, keepdims=False)
-    mine = jnp.transpose(mine.reshape(heads, group, rows), (1, 0, 2)).reshape(-1)
-    put, take = slots_of(mine, section, lax.rem(lane, parts) * section, total)
-    packed = jnp.stack([by_head(qk, side, heads), by_head(values, side, heads)], axis=1)
-    packed = lax.all_to_all(
-        packed, "seq", split_axis=0, concat_axis=0, tiled=True, axis_index_groups=along
-    )
-    tokens = lax.all_gather(packed, "seq", axis_index_groups=within)
-    tokens = tokens.reshape(shards, 2, rows, HEAD_DIM)
+    plan = (sides, shards, heads, sides, parts)
+    tokens, places = bring_in(qk, values, place.reshape(-1, HEAD_DIM), plan)
+    put, take = slots_of(places.reshape(-1), section, lax.rem(lane, parts) * section, total)
     out, lse = local_attend(put, take, tokens, section)
     out = lax.all_to_all(
         out, "seq", split_axis=0, concat_axis=0, tiled=True, axis_index_groups=within

time: 186 us -> 142 us (0.76)
  blocking collectives: 95.4 us -> 25.3 us
  Pallas kernels: 41.3 us -> 79.3 us
  between operations: 13.6 us -> 0.1 us
    all_gather x1 -> x0, blocking collectives: 40.3 us -> none  [by_heads_on_device(): lax.all_gather(place, ('round', 'seq')).reshape(sides, shards, rows)]
    pallas_call x0 -> x1, Pallas kernels: none -> 38 us  [bring_in(): pl.pallas_call(functools.partial(bring_kernel, plan), out_shape=(jax.Shap...]
    all_to_all x1 -> x0, blocking collectives: 31.9 us -> none  [by_heads_on_device(): lax.all_to_all(packed, 'seq', split_axis=0, concat_axis=0, tiled=True, ax...]
    unnamed x10 -> x8, local copies, waits for them, and re-layouts: 0.46 us -> 4.37 us
    all_to_all x1, blocking collectives: 16.9 us -> 19 us  [by_heads_on_device(): lax.all_to_all(merged, 'seq', split_axis=0, concat_axis=0, tiled=True, ax...]
  transfers between devices with their start and end apart: 2 -> 1, of which waited for: 1 -> 1; matrix products, arithmetic and copies ran while one was open for 0% -> 0% of each run, Pallas kernels for 0% -> 0%
where the time goes in v1:
time: 142 us
  Pallas kernels  79.3 us (56%)
  waiting for transfers between devices  25.4 us (18%)
  blocking collectives  25.3 us (18%)
  local copies, waits for them, and re-layouts  5.61 us (4%)
  starting transfers between devices  3.61 us (3%)
  other arithmetic  2.22 us (2%)
    pallas_call x1, Pallas kernels, local_attend(): pl.pallas_call(local_kernel, out_shape=(jax.ShapeDtypeStruct((blocks, row...  41.3 us
    pallas_call x1, Pallas kernels, bring_in(): pl.pallas_call(functools.partial(bring_kernel, plan), out_shape=(jax.Shap...  38 us
    all_to_all x1, waiting for transfers between devices, by_heads_on_device(): lax.all_to_all(out, 'seq', split_axis=0, concat_axis=0, tiled=True, axis_...  25.4 us
    all_to_all x1, blocking collectives, by_heads_on_device(): lax.all_to_all(merged, 'seq', split_axis=0, concat_axis=0, tiled=True, ax...  19 us
    all_to_all x1, blocking collectives, by_heads_on_device(): lax.all_to_all(lse, 'seq', split_axis=0, concat_axis=0, tiled=True, axis_...  6.36 us
    unnamed x8, local copies, waits for them, and re-layouts  4.37 us
    all_to_all x1, starting transfers between devices, by_heads_on_device(): lax.all_to_all(out, 'seq', split_axis=0, concat_axis=0, tiled=True, axis_...  3.61 us
  transfers between devices with their start and end apart: 1, of which 1 were waited for; matrix products, arithmetic and copies ran while one was open for 0% of the time, Pallas kernels for 0%

profile of v1, /device:TPU:0, one launch (start us, length us, event | category | flops | bytes accessed | tf_op | source)
XLA Modules:
  0.0 141.6 jit_solution(16635362675791693709)
XLA Ops:
  0.0 0.7 multiply_add_fusion
  0.7 0.0 copy-start.1
  0.7 1.2 copy-done.1
  1.9 0.0 copy-start.2
  1.9 1.2 copy-done.2
  3.2 38.0 %bring_in.1 = (bf16[16,2,512,128]{3,2,1,0:T(8,128)(2,1)S(1)}, s32[16,4,128]{2,1,0:T(4,128)S(1)}) custom-call(bf16[512,1024]{1,0:T(8,128)(2,1)S(1)} %copy-done.1, bf16[512,1024]{1,0:T(8,128)(2,1)S(1)} %copy-done.2, s32[4,128]{1,0:T(4,128)S(1)} %bitcast.11), custom_call_target="tpu_custom_call" | custom-call | tf_op jit(solution)/shard_map/bring_in/pallas_call | solution.py:402
  41.2 0.0 copy-start
  41.2 1.9 %copy-done = bf16[16,2,512,128]{3,2,1,0:T(8,128)(2,1)} copy-done((bf16[16,2,512,128]{3,2,1,0:T(8,128)(2,1)}, bf16[16,2,512,128]{3,2,1,0:T(8,128)(2,1)S(1)}, u32[]{:S(2)}) %copy-start) | copy-done | bytes 4194328
  43.1 41.3 %local_attend.1 = (bf16[16,512,128]{2,1,0:T(8,128)(2,1)}, f32[16,1,512]{2,1,0:T(1,128)S(1)}) custom-call(s32[8192]{0:T(1024)S(1)} %get-tuple-element.14.put_ref, s32[8192]{0:T(1024)S(1)} %get-tuple-element.13.take_ref, bf16[16,2,512,128]{3,2,1,0:T(8,128)(2,1)} %copy-done), custom_call_target="tpu_custom_call" | custom-call | tf_op jit(solution)/shard_map/local_attend/pallas_call | solution.py:214
  84.4 6.4 %all_to_all.15 = f32[16,1,512]{2,1,0:T(1,128)S(1)} all-to-all(f32[16,1,512]{2,1,0:T(1,128)S(1)} %get-tuple-element.11), channel_id=1, replica_groups={{0,1,2,3},{4,5,6,7},{8,9,10,11},{12,13,14,15},{16,17,18,19},{20,21,22,2..., dimensions={0} | all-to-all | bytes 65536 | tf_op jit(solution)/shard_map/all_to_all | solution.py:460
  90.8 3.6 %all-to-all-start.1 = ((bf16[16,512,128]{2,1,0:T(8,128)(2,1)}), bf16[16,512,128]{2,1,0:T(8,128)(2,1)S(1)}, u32[]{:S(2)}, u32[]{:S(2)}) async-start(bf16[16,512,128]{2,1,0:T(8,128)(2,1)} %get-tuple-element.12), calls=%async_computation.1 | async-start | bytes 4194304 | tf_op jit(solution)/shard_map/all_to_all | solution.py:457
  94.4 0.1 reduce
  94.6 25.4 %all-to-all-done.1 = bf16[16,512,128]{2,1,0:T(8,128)(2,1)S(1)} async-done(((bf16[16,512,128]{2,1,0:T(8,128)(2,1)}), bf16[16,512,128]{2,1,0:T(8,128)(2,1)S(1)}, u32[]{:S(2)}, u32[]{:S(2)}) %all-to-all-start.1) | async-done | bytes 2097184 | tf_op jit(solution)/shard_map/all_to_all | solution.py:457
  120.0 1.4 fusion
  121.4 19.0 %all_to_all.16 = bf16[4,512,128]{2,1,0:T(8,128)(2,1)S(1)} all-to-all(bf16[4,512,128]{2,1,0:T(8,128)(2,1)S(1)} %fusion), channel_id=1, replica_groups={{0,4,8,12},{1,5,9,13},{2,6,10,14},{3,7,11,15},{16,20,24,28},{17,21,25,2..., dimensions={0} | all-to-all | bytes 1048576 | tf_op jit(solution)/shard_map/all_to_all | solution.py:466
  140.4 0.2 copy.5
  140.6 1.0 copy.6
  (8 shorter events, 0.1 us)
Async XLA Ops:
  0.7 1.2 copy-start.1
  1.9 1.2 copy-start.2
  41.2 1.9 %copy-start = (bf16[16,2,512,128]{3,2,1,0:T(8,128)(2,1)}, bf16[16,2,512,128]{3,2,1,0:T(8,128)(2,1)S(1)}, u32[]{:S(2)}) copy-start(bf16[16,2,512,128]{3,2,1,0:T(8,128)(2,1)S(1)} %get-tuple-element.10.tokens_ref) | copy-start | bytes 12582916
  90.8 29.2 %all-to-all-start.1 = ((bf16[16,512,128]{2,1,0:T(8,128)(2,1)}), bf16[16,512,128]{2,1,0:T(8,128)(2,1)S(1)}, u32[]{:S(2)}, u32[]{:S(2)}) async-start(bf16[16,512,128]{2,1,0:T(8,128)(2,1)} %get-tuple-element.12), calls=%async_computation.1 | async-start | bytes 4194304 | tf_op jit(solution)/shard_map/all_to_all | solution.py:457

commit v2 on v1

--- a/solution.py
+++ b/solution.py
@@ -234,7 +234,7 @@
             pltpu.VMEM((bound, wide), jnp.float32),
             pltpu.VMEM((bound, wide), jnp.float32),
         ],
-        compiler_params=pltpu.CompilerParams(vmem_limit_bytes=48 * 1024 * 1024),
+        compiler_params=pltpu.CompilerParams(vmem_limit_bytes=24 * 1024 * 1024),
         name="local_attend",
     )(put, take, tokens)
 
@@ -425,11 +425,174 @@
     )(qk, values, place)
 
 
-def head_groups(shards, heads):
-    group = shards // heads
-    along = [[lane + group * step for step in range(heads)] for lane in range(group)]
-    within = [[group * step + lane for lane in range(group)] for step in range(heads)]
-    return group, along, within
+def send_kernel(
+    plan, part_ref, logs_ref, out_ref,
+    near_part, near_logs, far_part, far_logs, pass_part, pass_logs, done,
+    near_send, near_recv, near_log_send, near_log_recv,
+    far_send, far_recv, far_log_send, far_log_recv, line_send, line_recv,
+):
+    sides, shards, heads, fars, nears = plan
+    group = fars * nears
+    side, seat = lax.axis_index("round"), lax.axis_index("seq")
+    level, lane = seat // group, lax.rem(seat, group)
+    far, near = lane // nears, lax.rem(lane, nears)
+    rows = part_ref.shape[1]
+
+    def seat_of(level, far, near):
+        return level * group + far * nears + near
+
+    def block_of(level, far, near):
+        return (far * nears + near) * heads + level
+
+    def remote(source, target, send, recv, to):
+        return pltpu.make_async_remote_copy(
+            src_ref=source, dst_ref=target, send_sem=send, recv_sem=recv,
+            device_id=(side, to), device_id_type=MESH,
+        )
+
+    greet_all(sides, shards, side, seat)
+    steps = near_first(heads)[::-1] + [0]
+    aways = list(range(1, fars)) + [0]
+    sent = []
+    from_near, log_from_near = {}, {}
+    for away in aways:
+        for turn in range(1, nears):
+            to_near = lax.rem(near + turn, nears)
+            to = seat_of(level, far, to_near)
+            copy = remote(
+                logs_ref.at[pl.ds(block_of(0, lax.rem(far + away, fars), to_near), heads)],
+                near_logs.at[turn - 1, away],
+                near_log_send.at[turn - 1, away], near_log_recv.at[turn - 1, away], to,
+            )
+            copy.start()
+            sent.append(copy)
+            log_from_near[turn, away] = copy
+    for away in aways:
+        for step in steps:
+            for turn in range(1, nears):
+                to_near = lax.rem(near + turn, nears)
+                at = away * heads + step
+                copy = remote(
+                    part_ref.at[
+                        block_of(lax.rem(level + step, heads), lax.rem(far + away, fars), to_near)
+                    ],
+                    near_part.at[turn - 1, at],
+                    near_send.at[turn - 1, at], near_recv.at[turn - 1, at],
+                    seat_of(level, far, to_near),
+                )
+                copy.start()
+                sent.append(copy)
+                from_near[turn, at] = copy
+
+    def logs_here(away):
+        first = block_of(0, lax.rem(far + away, fars), near)
+        total = logs_ref[pl.ds(first, heads)]
+        for turn in range(1, nears):
+            log_from_near[turn, away].wait_recv()
+            total = jnp.maximum(total, near_logs[turn - 1, away])
+        return total
+
+    def part_here(away, step):
+        at = away * heads + step
+        total = part_ref[
+            block_of(lax.rem(level + step, heads), lax.rem(far + away, fars), near)
+        ].astype(jnp.float32)
+        for turn in range(1, nears):
+            from_near[turn, at].wait_recv()
+            total = total + near_part[turn - 1, at].astype(jnp.float32)
+        return total
+
+    from_far, log_from_far = {}, {}
+    for away in range(1, fars):
+        pass_logs[away] = logs_here(away)
+        copy = remote(
+            pass_logs.at[away], far_logs.at[away - 1],
+            far_log_send.at[away - 1], far_log_recv.at[away - 1],
+            seat_of(level, lax.rem(far + away, fars), near),
+        )
+        copy.start()
+        sent.append(copy)
+        log_from_far[away] = copy
+    pass_logs[0] = logs_here(0)
+    for away in range(1, fars):
+        for step in steps:
+            pass_part[away - 1, step] = part_here(away, step).astype(jnp.bfloat16)
+            copy = remote(
+                pass_part.at[away - 1, step], far_part.at[away - 1, step],
+                far_send.at[away - 1, step], far_recv.at[away - 1, step],
+                seat_of(level, lax.rem(far + away, fars), near),
+            )
+            copy.start()
+            sent.append(copy)
+            from_far[away, step] = copy
+
+    for away in range(1, fars):
+        log_from_far[away].wait_recv()
+
+    def spread(weight):
+        return jnp.transpose(jnp.broadcast_to(weight, (HEAD_DIM, rows)))
+
+    from_line = []
+    for step in steps:
+        to = lax.rem(level + step, heads)
+        logs = [pass_logs[0, to]] + [far_logs[away - 1, to] for away in range(1, fars)]
+        highest = functools.reduce(jnp.maximum, logs)
+        weights = [jnp.exp(log - highest) for log in logs]
+        total = functools.reduce(jnp.add, weights)
+        merged = spread(weights[0] / total) * part_here(0, step)
+        for away in range(1, fars):
+            share = spread(weights[away] / total)
+            from_far[away, step].wait_recv()
+            merged = merged + share * far_part[away - 1, step].astype(jnp.float32)
+        columns = pl.ds(pl.multiple_of(level * HEAD_DIM, HEAD_DIM), HEAD_DIM)
+        if step:
+            done[step - 1] = merged.astype(jnp.bfloat16)
+            copy = remote(
+                done.at[step - 1], out_ref.at[:, columns],
+                line_send.at[step - 1], line_recv.at[step - 1], seat_of(to, far, near),
+            )
+            copy.start()
+            sent.append(copy)
+            from_line.append(copy)
+        else:
+            out_ref[:, columns] = merged.astype(jnp.bfloat16)
+    for copy in from_line:
+        copy.wait_recv()
+    for copy in sent:
+        copy.wait_send()
+
+
+def send_back(part, logs, plan):
+    sides, shards, heads, fars, nears = plan
+    rows = part.shape[1]
+    dma = pltpu.SemaphoreType.DMA
+
+    def held(*lead):
+        return pltpu.VMEM(lead + (rows, HEAD_DIM), jnp.bfloat16)
+
+    def logs_held(*lead):
+        return pltpu.VMEM(lead + (heads, 1, rows), jnp.float32)
+
+    near_shape, far_shape = (nears - 1, fars * heads), (fars - 1, heads)
+    return pl.pallas_call(
+        functools.partial(send_kernel, plan),
+        out_shape=jax.ShapeDtypeStruct((rows, heads * HEAD_DIM), jnp.bfloat16),
+        in_specs=[pl.BlockSpec(memory_space=pltpu.VMEM)] * 2,
+        out_specs=pl.BlockSpec(memory_space=pltpu.VMEM),
+        scratch_shapes=[
+            held(*near_shape), logs_held(nears - 1, fars),
+            held(*far_shape), logs_held(fars - 1),
+            held(*far_shape), logs_held(fars),
+            held(heads - 1),
+            dma(near_shape), dma(near_shape), dma((nears - 1, fars)), dma((nears - 1, fars)),
+            dma(far_shape), dma(far_shape), dma((fars - 1,)), dma((fars - 1,)),
+            dma((heads - 1,)), dma((heads - 1,)),
+        ],
+        compiler_params=pltpu.CompilerParams(
+            collective_id=1, has_side_effects=True, vmem_limit_bytes=24 * 1024 * 1024
+        ),
+        name="send_back",
+    )(part, logs)
 
 
 def slots_of(place, section, base, total):
@@ -445,7 +608,7 @@
     rows, width = qk.shape
     heads = width // HEAD_DIM // sides
     total = rows * shards
-    group, along, within = head_groups(shards, heads)
+    group = shards // heads
     parts = group // sides
     section = total // parts
     lane = lax.rem(lax.axis_index("seq"), group)
@@ -453,20 +616,8 @@
     plan = (sides, shards, heads, sides, parts)
     tokens, places = bring_in(qk, values, place.reshape(-1, HEAD_DIM), plan)
     put, take = slots_of(places.reshape(-1), section, lax.rem(lane, parts) * section, total)
-    out, lse = local_attend(put, take, tokens, section)
-    out = lax.all_to_all(
-        out, "seq", split_axis=0, concat_axis=0, tiled=True, axis_index_groups=within
-    ).reshape(group, heads, rows, HEAD_DIM)
-    lse = lax.all_to_all(
-        lse, "seq", split_axis=0, concat_axis=0, tiled=True, axis_index_groups=within
-    ).reshape(group, heads, rows)
-    weight = jnp.exp(lse - jnp.max(lse, axis=0, keepdims=True))
-    weight = weight / jnp.sum(weight, axis=0, keepdims=True)
-    merged = jnp.sum(weight[..., None] * out.astype(jnp.float32), axis=0).astype(jnp.bfloat16)
-    merged = lax.all_to_all(
-        merged, "seq", split_axis=0, concat_axis=0, tiled=True, axis_index_groups=along
-    )
-    return jnp.transpose(merged, (1, 0, 2)).reshape(rows, heads * HEAD_DIM)
+    part, logs = local_attend(put, take, tokens, section)
+    return send_back(part, logs, plan)
 
 
 def whole_head_fits(qk, shards, sides):

time: 142 us -> 104 us (0.73)
  waiting for transfers between devices: 25.4 us -> 0 us
  blocking collectives: 25.3 us -> 0 us
  Pallas kernels: 79.3 us -> 99.9 us
  starting transfers between devices: 3.61 us -> 0 us
  local copies, waits for them, and re-layouts: 5.61 us -> 3.24 us
  other arithmetic: 2.22 us -> 0.73 us
    all_to_all x1 -> x0, waiting for transfers between devices: 25.4 us -> none  [by_heads_on_device(): lax.all_to_all(out, 'seq', split_axis=0, concat_axis=0, tiled=True, axis_...]
    all_to_all x2 -> x0, blocking collectives: 25.3 us -> none  [the longest x1 19 us: by_heads_on_device(): lax.all_to_all(merged, 'seq', split_axis=0, concat_axis=0, tiled=True, ax...]
    pallas_call x0 -> x1, Pallas kernels: none -> 22.5 us  [send_back(): pl.pallas_call(functools.partial(send_kernel, plan), out_shape=jax.ShapeD...]
    all_to_all x1 -> x0, starting transfers between devices: 3.61 us -> none  [by_heads_on_device(): lax.all_to_all(out, 'seq', split_axis=0, concat_axis=0, tiled=True, axis_...]
    pallas_call x1, Pallas kernels: 41.3 us -> 39.4 us  [local_attend(): pl.pallas_call(local_kernel, out_shape=(jax.ShapeDtypeStruct((blocks, row...]
    unnamed x8 -> x5, local copies, waits for them, and re-layouts: 4.37 us -> 3.24 us
  transfers between devices with their start and end apart: 1 -> 0, of which waited for: 1 -> 0; matrix products, arithmetic and copies ran while one was open for 0% -> 0% of each run, Pallas kernels for 0% -> 0%
where the time goes in v2:
time: 104 us
  Pallas kernels  99.9 us (96%)
  local copies, waits for them, and re-layouts  3.24 us (3%)
    pallas_call x1, Pallas kernels, local_attend(): pl.pallas_call(local_kernel, out_shape=(jax.ShapeDtypeStruct((blocks, row...  39.4 us
    pallas_call x1, Pallas kernels, bring_in(): pl.pallas_call(functools.partial(bring_kernel, plan), out_shape=(jax.Shap...  38 us
    pallas_call x1, Pallas kernels, send_back(): pl.pallas_call(functools.partial(send_kernel, plan), out_shape=jax.ShapeD...  22.5 us
    unnamed x5, local copies, waits for them, and re-layouts  3.24 us

profile of v2, /device:TPU:0, one launch (start us, length us, event | category | flops | bytes accessed | tf_op | source)
XLA Modules:
  0.0 104.0 jit_solution(7631493290888890904)
XLA Ops:
  0.0 0.7 multiply_add_fusion
  0.7 0.0 copy-start
  0.7 1.2 %copy-done = bf16[512,1024]{1,0:T(8,128)(2,1)S(1)} copy-done((bf16[512,1024]{1,0:T(8,128)(2,1)S(1)}, bf16[512,1024]{1,0:T(8,128)(2,1)}, u32[]{:S(2)}) %copy-start) | copy-done | bytes 1048600
  1.9 0.0 copy-start.1
  1.9 1.2 %copy-done.1 = bf16[512,1024]{1,0:T(8,128)(2,1)S(1)} copy-done((bf16[512,1024]{1,0:T(8,128)(2,1)S(1)}, bf16[512,1024]{1,0:T(8,128)(2,1)}, u32[]{:S(2)}) %copy-start.1) | copy-done | bytes 1048600
  3.2 38.0 %bring_in.1 = (bf16[16,2,512,128]{3,2,1,0:T(8,128)(2,1)S(1)}, s32[16,4,128]{2,1,0:T(4,128)S(1)}) custom-call(bf16[512,1024]{1,0:T(8,128)(2,1)S(1)} %copy-done, bf16[512,1024]{1,0:T(8,128)(2,1)S(1)} %copy-done.1, s32[4,128]{1,0:T(4,128)S(1)} %bitcast.2), custom_call_target="tpu_custom_call" | custom-call | tf_op jit(solution)/shard_map/bring_in/pallas_call | solution.py:402
  41.2 39.4 %local_attend.1 = (bf16[16,512,128]{2,1,0:T(8,128)(2,1)S(1)}, f32[16,1,512]{2,1,0:T(1,128)S(1)}) custom-call(s32[8192]{0:T(1024)S(1)} %get-tuple-element.14.put_ref, s32[8192]{0:T(1024)S(1)} %get-tuple-element.13.take_ref, bf16[16,2,512,128]{3,2,1,0:T(8,128)(2,1)S(1)} %get-tuple-element.10.tokens_ref), custom_call_target="tpu_custom_call" | custom-call | tf_op jit(solution)/shard_map/local_attend/pallas_call | solution.py:214
  80.6 22.5 %send_back.1 = bf16[512,512]{1,0:T(8,128)(2,1)S(1)} custom-call(bf16[16,512,128]{2,1,0:T(8,128)(2,1)S(1)} %get-tuple-element.11.part_ref, f32[16,1,512]{2,1,0:T(1,128)S(1)} %get-tuple-element.12.logs_ref), custom_call_target="tpu_custom_call" | custom-call | tf_op jit(solution)/shard_map/send_back/pallas_call | solution.py:577
  103.2 0.8 copy.6
  (2 shorter events, 0.0 us)
Async XLA Ops:
  0.7 1.2 %copy-start = (bf16[512,1024]{1,0:T(8,128)(2,1)S(1)}, bf16[512,1024]{1,0:T(8,128)(2,1)}, u32[]{:S(2)}) copy-start(bf16[512,1024]{1,0:T(8,128)(2,1)} %qk_ref.1) | copy-start | bytes 3145732
  1.9 1.2 %copy-start.1 = (bf16[512,1024]{1,0:T(8,128)(2,1)S(1)}, bf16[512,1024]{1,0:T(8,128)(2,1)}, u32[]{:S(2)}) copy-start(bf16[512,1024]{1,0:T(8,128)(2,1)} %values_ref.1) | copy-start | bytes 3145732

commit v3 on v2

--- a/solution.py
+++ b/solution.py
@@ -147,70 +147,88 @@
 
 
 NO_ROW = -1e30
-CHUNK = 16
-
-
-def local_kernel(
-    put_ref, take_ref, tokens_ref, out_ref, lse_ref, wide_q, wide_v, sorted_q, sorted_v, att, logs
-):
+STRIP = 128
+
+
+def local_kernel(put_ref, take_ref, tokens_ref, out_ref, lse_ref, wide, both, keys, vals):
     blocks, _, rows, _ = tokens_ref.shape
-    bound = sorted_q.shape[0] - 8
+    bound = keys.shape[0]
+    moves = put_ref.shape[1]
+    pairs = rows // moves
 
     @pl.loop(0, blocks)
     def _(block):
-        wide_q[...] = tokens_ref[block, 0].astype(jnp.float32)
-        wide_v[...] = tokens_ref[block, 1].astype(jnp.float32)
-
-        @pl.loop(0, rows, step=CHUNK)
-        def _(start):
-            for row in range(CHUNK):
-                to = put_ref[block * rows + start + row]
-                sorted_q[pl.ds(to, 1), :] = wide_q[pl.ds(start + row, 1), :]
-                sorted_v[pl.ds(to, 1), :] = wide_v[pl.ds(start + row, 1), :]
-
-    att[pl.ds(bound, 8), :] = jnp.zeros((8, HEAD_DIM), jnp.float32)
-    logs[pl.ds(bound, 8), :] = jnp.full((8, HEAD_DIM), NO_ROW, jnp.float32)
+        for k in range(2):
+            wide[pl.ds(k, rows, stride=2), :] = tokens_ref[block, k].astype(jnp.float32)
+
+        @pl.loop(0, pairs)
+        def _(group):
+            line = block * pairs + group
+            start = pl.multiple_of(group * (2 * moves), 2 * moves)
+            for row in range(moves):
+                to = put_ref[line, row]
+                both[pl.ds(to, 2), :] = wide[pl.ds(start + 2 * row, 2), :]
+
+    @pl.loop(0, bound // STRETCH)
+    def _(stretch):
+        low = pl.multiple_of(stretch * STRETCH, STRETCH)
+        field = both[pl.ds(2 * low, STRETCH, stride=2), :]
+        scale = lax.rsqrt(jnp.sum(field * field, axis=-1, keepdims=True) + eps_norm)
+        keys[pl.ds(low, STRETCH), :] = (field * scale).astype(jnp.bfloat16)
+        vals[pl.ds(low, STRETCH), :HEAD_DIM] = both[
+            pl.ds(2 * low + 1, STRETCH, stride=2), :
+        ].astype(jnp.bfloat16)
+        vals[pl.ds(low, STRETCH), HEAD_DIM:] = jnp.ones((STRETCH, HEAD_DIM), jnp.bfloat16)
+
+    row_at = lax.broadcasted_iota(jnp.int32, (STRIP, STRIP), 0)
+    col_at = lax.broadcasted_iota(jnp.int32, (STRIP, STRIP), 1)
 
     @pl.loop(0, bound // STRETCH - 1)
     def _(stretch):
         low = pl.multiple_of(stretch * STRETCH, STRETCH)
-        own = pl.multiple_of(low + STRETCH, STRETCH)
-        queries = sorted_q[pl.ds(own, STRETCH), :].astype(jnp.bfloat16)
-        field = sorted_q[pl.ds(low, 2 * STRETCH), :]
-        scale = lax.rsqrt(jnp.sum(field * field, axis=-1, keepdims=True) + eps_norm)
-        keys = (field * scale).astype(jnp.bfloat16)
-        vals = sorted_v[pl.ds(low, 2 * STRETCH), :].astype(jnp.bfloat16)
-        scores = lax.dot_general(
-            queries, keys, (((1,), (1,)), ((), ())), preferred_element_type=jnp.float32
-        )
-        row_at = lax.broadcasted_iota(jnp.int32, scores.shape, 0) + STRETCH
-        col_at = lax.broadcasted_iota(jnp.int32, scores.shape, 1)
-        scores = jnp.where(row_at == col_at, jnp.float32(self_score), scores)
-        highest = jnp.max(scores, axis=-1, keepdims=True)
-        probs = jnp.exp(scores - highest)
-        weight = jnp.sum(probs, axis=-1, keepdims=True)
-        attended = jnp.dot(probs.astype(jnp.bfloat16), vals, preferred_element_type=jnp.float32)
-        att[pl.ds(own, STRETCH), :] = attended / weight
-        logs[pl.ds(own, STRETCH), :] = jnp.broadcast_to(
-            highest + jnp.log(weight), (STRETCH, HEAD_DIM)
-        )
+        window = keys[pl.ds(low, 2 * STRETCH), :]
+        seen = vals[pl.ds(low, 2 * STRETCH), :]
+        for strip in range(0, STRETCH, STRIP):
+            at = 2 * (low + STRETCH + strip)
+            queries = both[pl.ds(at, STRIP, stride=2), :].astype(jnp.bfloat16)
+            scores = lax.dot_general(
+                queries, window, (((1,), (1,)), ((), ())), preferred_element_type=jnp.float32
+            )
+            left, right = STRETCH + strip, STRETCH + strip + STRIP
+            pieces = [
+                scores[:, :left],
+                jnp.where(row_at == col_at, jnp.float32(self_score), scores[:, left:right]),
+            ]
+            if right < 2 * STRETCH:
+                pieces.append(scores[:, right:])
+            scores = jnp.concatenate(pieces, axis=1)
+            highest = jnp.max(scores, axis=-1, keepdims=True)
+            probs = jnp.exp(scores - highest).astype(jnp.bfloat16)
+            summed = jnp.dot(probs, seen, preferred_element_type=jnp.float32)
+            weight = summed[:, HEAD_DIM:]
+            both[pl.ds(at, STRIP, stride=2), :] = summed[:, :HEAD_DIM] / weight
+            both[pl.ds(at + 1, STRIP, stride=2), :] = highest + jnp.log(weight)
+
+    parity = lax.rem(lax.broadcasted_iota(jnp.int32, (8, HEAD_DIM), 0), 2)
+    both[pl.ds(2 * bound, 8), :] = jnp.where(parity == 0, 0.0, NO_ROW).astype(jnp.float32)
 
     @pl.loop(0, blocks)
     def _(block):
-        @pl.loop(0, rows, step=CHUNK)
-        def _(start):
-            for row in range(CHUNK):
-                at = take_ref[block * rows + start + row]
-                wide_q[pl.ds(start + row, 1), :] = att[pl.ds(at, 1), :]
-                wide_v[pl.ds(start + row, 1), :] = logs[pl.ds(at, 1), :]
-
-        out_ref[block] = wide_q[...].astype(jnp.bfloat16)
-        lse_ref[block] = jnp.transpose(wide_v[...])[0:1, :]
+        @pl.loop(0, pairs)
+        def _(group):
+            line = block * pairs + group
+            start = pl.multiple_of(group * (2 * moves), 2 * moves)
+            for row in range(moves):
+                at = take_ref[line, row]
+                wide[pl.ds(start + 2 * row, 2), :] = both[pl.ds(at, 2), :]
+
+        out_ref[block] = wide[pl.ds(0, rows, stride=2), :].astype(jnp.bfloat16)
+        lse_ref[block] = jnp.transpose(wide[pl.ds(1, rows, stride=2), :])[0:1, :]
 
 
 def local_attend(put, take, tokens, section):
     blocks, _, rows, wide = tokens.shape
-    bound = section + STRETCH + 8
+    bound = section + STRETCH
     return pl.pallas_call(
         local_kernel,
         out_shape=(
@@ -227,12 +245,10 @@
             pl.BlockSpec(memory_space=pltpu.VMEM),
         ),
         scratch_shapes=[
-            pltpu.VMEM((rows, wide), jnp.float32),
-            pltpu.VMEM((rows, wide), jnp.float32),
-            pltpu.VMEM((bound, wide), jnp.float32),
-            pltpu.VMEM((bound, wide), jnp.float32),
-            pltpu.VMEM((bound, wide), jnp.float32),
-            pltpu.VMEM((bound, wide), jnp.float32),
+            pltpu.VMEM((2 * rows, wide), jnp.float32),
+            pltpu.VMEM((2 * bound + 8, wide), jnp.float32),
+            pltpu.VMEM((bound, wide), jnp.bfloat16),
+            pltpu.VMEM((bound, 2 * wide), jnp.bfloat16),
         ],
         compiler_params=pltpu.CompilerParams(vmem_limit_bytes=24 * 1024 * 1024),
         name="local_attend",
@@ -405,7 +421,7 @@
             jax.ShapeDtypeStruct((shards, 2, rows, HEAD_DIM), jnp.bfloat16),
             jax.ShapeDtypeStruct((shards,) + place.shape, jnp.int32),
         ),
-        in_specs=[pl.BlockSpec(memory_space=pltpu.VMEM)] * 3,
+        in_specs=[pl.BlockSpec(memory_space=pltpu.HBM)] * 2 + [pl.BlockSpec(memory_space=pltpu.VMEM)],
         out_specs=(pl.BlockSpec(memory_space=pl.ANY), pl.BlockSpec(memory_space=pl.ANY)),
         scratch_shapes=[
             dma((2,)),
@@ -599,7 +615,7 @@
     bound = section + STRETCH
     put = jnp.minimum(lax.rem(place - base + STRETCH + total, total), bound)
     take = jnp.where(put < STRETCH, bound, put)
-    return put, take
+    return 2 * put, 2 * take
 
 
 def by_heads_on_device(qk, values, dest_dev, dest_slot):
@@ -615,7 +631,7 @@
     place = dest_dev[0] * rows + dest_slot[0]
     plan = (sides, shards, heads, sides, parts)
     tokens, places = bring_in(qk, values, place.reshape(-1, HEAD_DIM), plan)
-    put, take = slots_of(places.reshape(-1), section, lax.rem(lane, parts) * section, total)
+    put, take = slots_of(places.reshape(-1, HEAD_DIM), section, lax.rem(lane, parts) * section, total)
     part, logs = local_attend(put, take, tokens, section)
     return send_back(part, logs, plan)
 

time: 104 us -> 92.2 us (0.89)
  Pallas kernels: 99.9 us -> 88 us
    pallas_call x1, Pallas kernels: 39.4 us -> 27.5 us  [local_attend(): pl.pallas_call(local_kernel, out_shape=(jax.ShapeDtypeStruct((blocks, row...]
where the time goes in v3:
time: 92.2 us; the launch traced here: 92 us
  Pallas kernels  88 us (95%)
  local copies, waits for them, and re-layouts  3.24 us (4%)
    pallas_call x1, Pallas kernels, bring_in(): pl.pallas_call(functools.partial(bring_kernel, plan), out_shape=(jax.Shap...  38 us
    pallas_call x1, Pallas kernels, local_attend(): pl.pallas_call(local_kernel, out_shape=(jax.ShapeDtypeStruct((blocks, row...  27.5 us
    pallas_call x1, Pallas kernels, send_back(): pl.pallas_call(functools.partial(send_kernel, plan), out_shape=jax.ShapeD...  22.5 us
    unnamed x5, local copies, waits for them, and re-layouts  3.24 us

profile of v3, /device:TPU:0, one launch (start us, length us, event | category | flops | bytes accessed | tf_op | source)
XLA Modules:
  0.0 92.0 jit_solution(13980257346245455570)
XLA Ops:
  0.0 0.7 multiply_add_fusion
  0.7 0.0 copy-start
  0.7 1.2 %copy-done = bf16[512,1024]{1,0:T(8,128)(2,1)S(1)} copy-done((bf16[512,1024]{1,0:T(8,128)(2,1)S(1)}, bf16[512,1024]{1,0:T(8,128)(2,1)}, u32[]{:S(2)}) %copy-start) | copy-done | bytes 1048600
  1.9 0.0 copy-start.1
  1.9 1.2 %copy-done.1 = bf16[512,1024]{1,0:T(8,128)(2,1)S(1)} copy-done((bf16[512,1024]{1,0:T(8,128)(2,1)S(1)}, bf16[512,1024]{1,0:T(8,128)(2,1)}, u32[]{:S(2)}) %copy-start.1) | copy-done | bytes 1048600
  3.2 38.0 %bring_in.1 = (bf16[16,2,512,128]{3,2,1,0:T(8,128)(2,1)S(1)}, s32[16,4,128]{2,1,0:T(4,128)S(1)}) custom-call(bf16[512,1024]{1,0:T(8,128)(2,1)S(1)} %copy-done, bf16[512,1024]{1,0:T(8,128)(2,1)S(1)} %copy-done.1, s32[4,128]{1,0:T(4,128)S(1)} %bitcast.2), custom_call_target="tpu_custom_call" | custom-call | tf_op jit(solution)/shard_map/bring_in/pallas_call | solution.py:418
  41.2 27.5 %local_attend.1 = (bf16[16,512,128]{2,1,0:T(8,128)(2,1)S(1)}, f32[16,1,512]{2,1,0:T(1,128)S(1)}) custom-call(s32[64,128]{1,0:T(8,128)S(1)} %get-tuple-element.14.put_ref, s32[64,128]{1,0:T(8,128)S(1)} %get-tuple-element.13.take_ref, bf16[16,2,512,128]{3,2,1,0:T(8,128)(2,1)S(1)} %get-tuple-element.10.tokens_ref), custom_call_target="tpu_custom_call" | custom-call | tf_op jit(solution)/shard_map/local_attend/pallas_call | solution.py:232
  68.7 22.5 %send_back.1 = bf16[512,512]{1,0:T(8,128)(2,1)S(1)} custom-call(bf16[16,512,128]{2,1,0:T(8,128)(2,1)S(1)} %get-tuple-element.11.part_ref, f32[16,1,512]{2,1,0:T(1,128)S(1)} %get-tuple-element.12.logs_ref), custom_call_target="tpu_custom_call" | custom-call | tf_op jit(solution)/shard_map/send_back/pallas_call | solution.py:593
  91.2 0.8 copy.6
  (2 shorter events, 0.0 us)
Async XLA Ops:
  0.7 1.2 %copy-start = (bf16[512,1024]{1,0:T(8,128)(2,1)S(1)}, bf16[512,1024]{1,0:T(8,128)(2,1)}, u32[]{:S(2)}) copy-start(bf16[512,1024]{1,0:T(8,128)(2,1)} %qk_ref.1) | copy-start | bytes 3145732
  1.9 1.2 %copy-start.1 = (bf16[512,1024]{1,0:T(8,128)(2,1)S(1)}, bf16[512,1024]{1,0:T(8,128)(2,1)}, u32[]{:S(2)}) copy-start(bf16[512,1024]{1,0:T(8,128)(2,1)} %values_ref.1) | copy-start | bytes 3145732

commit v4 on v3

--- a/solution.py
+++ b/solution.py
@@ -150,7 +150,7 @@
 STRIP = 128
 
 
-def local_kernel(put_ref, take_ref, tokens_ref, out_ref, lse_ref, wide, both, keys, vals):
+def local_kernel(put_ref, tokens_ref, both, wide, keys, vals):
     blocks, _, rows, _ = tokens_ref.shape
     bound = keys.shape[0]
     moves = put_ref.shape[1]
@@ -212,47 +212,26 @@
     parity = lax.rem(lax.broadcasted_iota(jnp.int32, (8, HEAD_DIM), 0), 2)
     both[pl.ds(2 * bound, 8), :] = jnp.where(parity == 0, 0.0, NO_ROW).astype(jnp.float32)
 
-    @pl.loop(0, blocks)
-    def _(block):
-        @pl.loop(0, pairs)
-        def _(group):
-            line = block * pairs + group
-            start = pl.multiple_of(group * (2 * moves), 2 * moves)
-            for row in range(moves):
-                at = take_ref[line, row]
-                wide[pl.ds(start + 2 * row, 2), :] = both[pl.ds(at, 2), :]
-
-        out_ref[block] = wide[pl.ds(0, rows, stride=2), :].astype(jnp.bfloat16)
-        lse_ref[block] = jnp.transpose(wide[pl.ds(1, rows, stride=2), :])[0:1, :]
-
-
-def local_attend(put, take, tokens, section):
-    blocks, _, rows, wide = tokens.shape
+
+def local_attend(put, tokens, section):
+    rows, wide = tokens.shape[2:]
     bound = section + STRETCH
     return pl.pallas_call(
         local_kernel,
-        out_shape=(
-            jax.ShapeDtypeStruct((blocks, rows, wide), jnp.bfloat16),
-            jax.ShapeDtypeStruct((blocks, 1, rows), jnp.float32),
-        ),
+        out_shape=jax.ShapeDtypeStruct((2 * bound + 8, wide), jnp.float32),
         in_specs=[
-            pl.BlockSpec(memory_space=pltpu.SMEM),
             pl.BlockSpec(memory_space=pltpu.SMEM),
             pl.BlockSpec(memory_space=pltpu.VMEM),
         ],
-        out_specs=(
-            pl.BlockSpec(memory_space=pltpu.VMEM),
-            pl.BlockSpec(memory_space=pltpu.VMEM),
-        ),
+        out_specs=pl.BlockSpec(memory_space=pltpu.VMEM),
         scratch_shapes=[
             pltpu.VMEM((2 * rows, wide), jnp.float32),
-            pltpu.VMEM((2 * bound + 8, wide), jnp.float32),
             pltpu.VMEM((bound, wide), jnp.bfloat16),
             pltpu.VMEM((bound, 2 * wide), jnp.bfloat16),
         ],
         compiler_params=pltpu.CompilerParams(vmem_limit_bytes=24 * 1024 * 1024),
         name="local_attend",
-    )(put, take, tokens)
+    )(put, tokens)
 
 
 MESH = pl.DeviceIdType.MESH
@@ -442,8 +421,8 @@
 
 
 def send_kernel(
-    plan, part_ref, logs_ref, out_ref,
-    near_part, near_logs, far_part, far_logs, pass_part, pass_logs, done,
+    plan, take_ref, both_ref, out_ref,
+    wide, part_ref, logs_ref, near_part, near_logs, far_part, far_logs, pass_part, pass_logs, done,
     near_send, near_recv, near_log_send, near_log_recv,
     far_send, far_recv, far_log_send, far_log_recv, line_send, line_recv,
 ):
@@ -453,6 +432,20 @@
     level, lane = seat // group, lax.rem(seat, group)
     far, near = lane // nears, lax.rem(lane, nears)
     rows = part_ref.shape[1]
+    moves = take_ref.shape[1]
+    pairs = rows // moves
+
+    def unsort(block):
+        @pl.loop(0, pairs)
+        def _(group):
+            line = block * pairs + group
+            start = pl.multiple_of(group * (2 * moves), 2 * moves)
+            for row in range(moves):
+                at = take_ref[line, row]
+                wide[pl.ds(start + 2 * row, 2), :] = both_ref[pl.ds(at, 2), :]
+
+        part_ref[block] = wide[pl.ds(0, rows, stride=2), :].astype(jnp.bfloat16)
+        logs_ref[block] = jnp.transpose(wide[pl.ds(1, rows, stride=2), :])[0:1, :]
 
     def seat_of(level, far, near):
         return level * group + far * nears + near
@@ -468,37 +461,32 @@
 
     greet_all(sides, shards, side, seat)
     steps = near_first(heads)[::-1] + [0]
-    aways = list(range(1, fars)) + [0]
     sent = []
     from_near, log_from_near = {}, {}
-    for away in aways:
+
+    def send_near(away):
         for turn in range(1, nears):
             to_near = lax.rem(near + turn, nears)
             to = seat_of(level, far, to_near)
-            copy = remote(
-                logs_ref.at[pl.ds(block_of(0, lax.rem(far + away, fars), to_near), heads)],
-                near_logs.at[turn - 1, away],
-                near_log_send.at[turn - 1, away], near_log_recv.at[turn - 1, away], to,
-            )
-            copy.start()
-            sent.append(copy)
-            log_from_near[turn, away] = copy
-    for away in aways:
-        for step in steps:
-            for turn in range(1, nears):
-                to_near = lax.rem(near + turn, nears)
+            first = block_of(0, lax.rem(far + away, fars), to_near)
+            for step in steps:
                 at = away * heads + step
+                block = first + lax.rem(level + step, heads)
+                unsort(block)
                 copy = remote(
-                    part_ref.at[
-                        block_of(lax.rem(level + step, heads), lax.rem(far + away, fars), to_near)
-                    ],
-                    near_part.at[turn - 1, at],
-                    near_send.at[turn - 1, at], near_recv.at[turn - 1, at],
-                    seat_of(level, far, to_near),
+                    part_ref.at[block], near_part.at[turn - 1, at],
+                    near_send.at[turn - 1, at], near_recv.at[turn - 1, at], to,
                 )
                 copy.start()
                 sent.append(copy)
                 from_near[turn, at] = copy
+            copy = remote(
+                logs_ref.at[pl.ds(first, heads)], near_logs.at[turn - 1, away],
+                near_log_send.at[turn - 1, away], near_log_recv.at[turn - 1, away], to,
+            )
+            copy.start()
+            sent.append(copy)
+            log_from_near[turn, away] = copy
 
     def logs_here(away):
         first = block_of(0, lax.rem(far + away, fars), near)
@@ -510,9 +498,9 @@
 
     def part_here(away, step):
         at = away * heads + step
-        total = part_ref[
-            block_of(lax.rem(level + step, heads), lax.rem(far + away, fars), near)
-        ].astype(jnp.float32)
+        block = block_of(lax.rem(level + step, heads), lax.rem(far + away, fars), near)
+        unsort(block)
+        total = part_ref[block].astype(jnp.float32)
         for turn in range(1, nears):
             from_near[turn, at].wait_recv()
             total = total + near_part[turn - 1, at].astype(jnp.float32)
@@ -520,27 +508,29 @@
 
     from_far, log_from_far = {}, {}
     for away in range(1, fars):
+        send_near(away)
+        to = seat_of(level, lax.rem(far + away, fars), near)
+        for step in steps:
+            pass_part[away - 1, step] = part_here(away, step).astype(jnp.bfloat16)
+            copy = remote(
+                pass_part.at[away - 1, step], far_part.at[away - 1, step],
+                far_send.at[away - 1, step], far_recv.at[away - 1, step], to,
+            )
+            copy.start()
+            sent.append(copy)
+            from_far[away, step] = copy
         pass_logs[away] = logs_here(away)
         copy = remote(
             pass_logs.at[away], far_logs.at[away - 1],
-            far_log_send.at[away - 1], far_log_recv.at[away - 1],
-            seat_of(level, lax.rem(far + away, fars), near),
+            far_log_send.at[away - 1], far_log_recv.at[away - 1], to,
         )
         copy.start()
         sent.append(copy)
         log_from_far[away] = copy
+    send_near(0)
+    for step in steps:
+        pass_part[fars - 1, step] = part_here(0, step).astype(jnp.bfloat16)
     pass_logs[0] = logs_here(0)
-    for away in range(1, fars):
-        for step in steps:
-            pass_part[away - 1, step] = part_here(away, step).astype(jnp.bfloat16)
-            copy = remote(
-                pass_part.at[away - 1, step], far_part.at[away - 1, step],
-                far_send.at[away - 1, step], far_recv.at[away - 1, step],
-                seat_of(level, lax.rem(far + away, fars), near),
-            )
-            copy.start()
-            sent.append(copy)
-            from_far[away, step] = copy
 
     for away in range(1, fars):
         log_from_far[away].wait_recv()
@@ -555,7 +545,7 @@
         highest = functools.reduce(jnp.maximum, logs)
         weights = [jnp.exp(log - highest) for log in logs]
         total = functools.reduce(jnp.add, weights)
-        merged = spread(weights[0] / total) * part_here(0, step)
+        merged = spread(weights[0] / total) * pass_part[fars - 1, step].astype(jnp.float32)
         for away in range(1, fars):
             share = spread(weights[away] / total)
             from_far[away, step].wait_recv()
@@ -578,9 +568,8 @@
         copy.wait_send()
 
 
-def send_back(part, logs, plan):
+def send_back(take, both, rows, plan):
     sides, shards, heads, fars, nears = plan
-    rows = part.shape[1]
     dma = pltpu.SemaphoreType.DMA
 
     def held(*lead):
@@ -593,12 +582,17 @@
     return pl.pallas_call(
         functools.partial(send_kernel, plan),
         out_shape=jax.ShapeDtypeStruct((rows, heads * HEAD_DIM), jnp.bfloat16),
-        in_specs=[pl.BlockSpec(memory_space=pltpu.VMEM)] * 2,
+        in_specs=[
+            pl.BlockSpec(memory_space=pltpu.SMEM),
+            pl.BlockSpec(memory_space=pltpu.VMEM),
+        ],
         out_specs=pl.BlockSpec(memory_space=pltpu.VMEM),
         scratch_shapes=[
+            pltpu.VMEM((2 * rows, HEAD_DIM), jnp.float32),
+            held(shards), pltpu.VMEM((shards, 1, rows), jnp.float32),
             held(*near_shape), logs_held(nears - 1, fars),
             held(*far_shape), logs_held(fars - 1),
-            held(*far_shape), logs_held(fars),
+            held(fars, heads), logs_held(fars),
             held(heads - 1),
             dma(near_shape), dma(near_shape), dma((nears - 1, fars)), dma((nears - 1, fars)),
             dma(far_shape), dma(far_shape), dma((fars - 1,)), dma((fars - 1,)),
@@ -608,7 +602,7 @@
             collective_id=1, has_side_effects=True, vmem_limit_bytes=24 * 1024 * 1024
         ),
         name="send_back",
-    )(part, logs)
+    )(take, both)
 
 
 def slots_of(place, section, base, total):
@@ -632,8 +626,8 @@
     plan = (sides, shards, heads, sides, parts)
     tokens, places = bring_in(qk, values, place.reshape(-1, HEAD_DIM), plan)
     put, take = slots_of(places.reshape(-1, HEAD_DIM), section, lax.rem(lane, parts) * section, total)
-    part, logs = local_attend(put, take, tokens, section)
-    return send_back(part, logs, plan)
+    both = local_attend(put, tokens, section)
+    return send_back(take, both, rows, plan)
 
 
 def whole_head_fits(qk, shards, sides):

time: 92.2 us -> 92.9 us (level)
    pallas_call x1, Pallas kernels: 22.5 us -> 32.4 us  [send_back(): pl.pallas_call(functools.partial(send_kernel, plan), out_shape=jax.ShapeD...]
    pallas_call x1, Pallas kernels: 27.5 us -> 18.2 us  [local_attend(): pl.pallas_call(local_kernel, out_shape=jax.ShapeDtypeStruct((2 * bound +...]
where the time goes in v4:
time: 92.9 us; the launch traced here: 92.7 us
  Pallas kernels  88.7 us (95%)
  local copies, waits for them, and re-layouts  3.24 us (3%)
    pallas_call x1, Pallas kernels, bring_in(): pl.pallas_call(functools.partial(bring_kernel, plan), out_shape=(jax.Shap...  38 us
    pallas_call x1, Pallas kernels, send_back(): pl.pallas_call(functools.partial(send_kernel, plan), out_shape=jax.ShapeD...  32.4 us
    pallas_call x1, Pallas kernels, local_attend(): pl.pallas_call(local_kernel, out_shape=jax.ShapeDtypeStruct((2 * bound +...  18.2 us
    unnamed x5, local copies, waits for them, and re-layouts  3.24 us

profile of v4, /device:TPU:0, one launch (start us, length us, event | category | flops | bytes accessed | tf_op | source)
XLA Modules:
  0.0 92.7 jit_solution(6193915311037416471)
XLA Ops:
  0.0 0.7 multiply_add_fusion
  0.7 0.0 copy-start
  0.7 1.2 %copy-done = bf16[512,1024]{1,0:T(8,128)(2,1)S(1)} copy-done((bf16[512,1024]{1,0:T(8,128)(2,1)S(1)}, bf16[512,1024]{1,0:T(8,128)(2,1)}, u32[]{:S(2)}) %copy-start) | copy-done | bytes 1048600
  1.9 0.0 copy-start.1
  1.9 1.2 %copy-done.1 = bf16[512,1024]{1,0:T(8,128)(2,1)S(1)} copy-done((bf16[512,1024]{1,0:T(8,128)(2,1)S(1)}, bf16[512,1024]{1,0:T(8,128)(2,1)}, u32[]{:S(2)}) %copy-start.1) | copy-done | bytes 1048600
  3.2 38.0 %bring_in.1 = (bf16[16,2,512,128]{3,2,1,0:T(8,128)(2,1)S(1)}, s32[16,4,128]{2,1,0:T(4,128)S(1)}) custom-call(bf16[512,1024]{1,0:T(8,128)(2,1)S(1)} %copy-done, bf16[512,1024]{1,0:T(8,128)(2,1)S(1)} %copy-done.1, s32[4,128]{1,0:T(4,128)S(1)} %bitcast.2), custom_call_target="tpu_custom_call" | custom-call | tf_op jit(solution)/shard_map/bring_in/pallas_call | solution.py:397
  41.2 18.2 %local_attend.1.both_ref = f32[9224,128]{1,0:T(8,128)S(1)} custom-call(s32[64,128]{1,0:T(8,128)S(1)} %get-tuple-element.9.put_ref, bf16[16,2,512,128]{3,2,1,0:T(8,128)(2,1)S(1)} %get-tuple-element.8.tokens_ref), custom_call_target="tpu_custom_call" | custom-call | tf_op jit(solution)/shard_map/local_attend/pallas_call | solution.py:219
  59.4 32.4 %send_back.1 = bf16[512,512]{1,0:T(8,128)(2,1)S(1)} custom-call(s32[64,128]{1,0:T(8,128)S(1)} %get-tuple-element.10.take_ref, f32[9224,128]{1,0:T(8,128)S(1)} %local_attend.1.both_ref), custom_call_target="tpu_custom_call" | custom-call | tf_op jit(solution)/shard_map/send_back/pallas_call | solution.py:582
  91.9 0.8 copy.6
  (2 shorter events, 0.0 us)
Async XLA Ops:
  0.7 1.2 %copy-start = (bf16[512,1024]{1,0:T(8,128)(2,1)S(1)}, bf16[512,1024]{1,0:T(8,128)(2,1)}, u32[]{:S(2)}) copy-start(bf16[512,1024]{1,0:T(8,128)(2,1)} %qk_ref.1) | copy-start | bytes 3145732
  1.9 1.2 %copy-start.1 = (bf16[512,1024]{1,0:T(8,128)(2,1)S(1)}, bf16[512,1024]{1,0:T(8,128)(2,1)}, u32[]{:S(2)}) copy-start(bf16[512,1024]{1,0:T(8,128)(2,1)} %values_ref.1) | copy-start | bytes 3145732

commit v5 on v4

--- a/solution.py
+++ b/solution.py
@@ -462,78 +462,65 @@
     greet_all(sides, shards, side, seat)
     steps = near_first(heads)[::-1] + [0]
     sent = []
-    from_near, log_from_near = {}, {}
-
-    def send_near(away):
+    from_near, from_far = {}, {}
+
+    def start(*copies):
+        for copy in copies:
+            copy.start()
+            sent.append(copy)
+        return copies
+
+    def send_near(away, step):
+        at = away * heads + step
         for turn in range(1, nears):
             to_near = lax.rem(near + turn, nears)
             to = seat_of(level, far, to_near)
-            first = block_of(0, lax.rem(far + away, fars), to_near)
-            for step in steps:
-                at = away * heads + step
-                block = first + lax.rem(level + step, heads)
-                unsort(block)
-                copy = remote(
+            block = block_of(lax.rem(level + step, heads), lax.rem(far + away, fars), to_near)
+            unsort(block)
+            from_near[turn, at] = start(
+                remote(
                     part_ref.at[block], near_part.at[turn - 1, at],
                     near_send.at[turn - 1, at], near_recv.at[turn - 1, at], to,
-                )
-                copy.start()
-                sent.append(copy)
-                from_near[turn, at] = copy
-            copy = remote(
-                logs_ref.at[pl.ds(first, heads)], near_logs.at[turn - 1, away],
-                near_log_send.at[turn - 1, away], near_log_recv.at[turn - 1, away], to,
-            )
-            copy.start()
-            sent.append(copy)
-            log_from_near[turn, away] = copy
-
-    def logs_here(away):
-        first = block_of(0, lax.rem(far + away, fars), near)
-        total = logs_ref[pl.ds(first, heads)]
-        for turn in range(1, nears):
-            log_from_near[turn, away].wait_recv()
-            total = jnp.maximum(total, near_logs[turn - 1, away])
-        return total
-
-    def part_here(away, step):
+                ),
+                remote(
+                    logs_ref.at[block], near_logs.at[turn - 1, at],
+                    near_log_send.at[turn - 1, at], near_log_recv.at[turn - 1, at], to,
+                ),
+            )
+
+    def here(away, step):
         at = away * heads + step
         block = block_of(lax.rem(level + step, heads), lax.rem(far + away, fars), near)
         unsort(block)
-        total = part_ref[block].astype(jnp.float32)
+        part = part_ref[block].astype(jnp.float32)
+        log = logs_ref[block]
         for turn in range(1, nears):
-            from_near[turn, at].wait_recv()
-            total = total + near_part[turn - 1, at].astype(jnp.float32)
-        return total
-
-    from_far, log_from_far = {}, {}
+            for copy in from_near[turn, at]:
+                copy.wait_recv()
+            part = part + near_part[turn - 1, at].astype(jnp.float32)
+            log = jnp.maximum(log, near_logs[turn - 1, at])
+        return part, log
+
     for away in range(1, fars):
-        send_near(away)
         to = seat_of(level, lax.rem(far + away, fars), near)
         for step in steps:
-            pass_part[away - 1, step] = part_here(away, step).astype(jnp.bfloat16)
-            copy = remote(
-                pass_part.at[away - 1, step], far_part.at[away - 1, step],
-                far_send.at[away - 1, step], far_recv.at[away - 1, step], to,
-            )
-            copy.start()
-            sent.append(copy)
-            from_far[away, step] = copy
-        pass_logs[away] = logs_here(away)
-        copy = remote(
-            pass_logs.at[away], far_logs.at[away - 1],
-            far_log_send.at[away - 1], far_log_recv.at[away - 1], to,
-        )
-        copy.start()
-        sent.append(copy)
-        log_from_far[away] = copy
-    send_near(0)
+            send_near(away, step)
+        for step in steps:
+            part, log = here(away, step)
+            pass_part[away - 1, step] = part.astype(jnp.bfloat16)
+            pass_logs[away - 1, step] = log
+            from_far[away, step] = start(
+                remote(
+                    pass_part.at[away - 1, step], far_part.at[away - 1, step],
+                    far_send.at[away - 1, step], far_recv.at[away - 1, step], to,
+                ),
+                remote(
+                    pass_logs.at[away - 1, step], far_logs.at[away - 1, step],
+                    far_log_send.at[away - 1, step], far_log_recv.at[away - 1, step], to,
+                ),
+            )
     for step in steps:
-        pass_part[fars - 1, step] = part_here(0, step).astype(jnp.bfloat16)
-    pass_logs[0] = logs_here(0)
-
-    for away in range(1, fars):
-        log_from_far[away].wait_recv()
+        send_near(0, step)
 
     def spread(weight):
         return jnp.transpose(jnp.broadcast_to(weight, (HEAD_DIM, rows)))
@@ -541,15 +528,19 @@
     from_line = []
     for step in steps:
         to = lax.rem(level + step, heads)
-        logs = [pass_logs[0, to]] + [far_logs[away - 1, to] for away in range(1, fars)]
+        part, log = here(0, step)
+        parts, logs = [part], [log]
+        for away in range(1, fars):
+            for copy in from_far[away, step]:
+                copy.wait_recv()
+            parts.append(far_part[away - 1, step].astype(jnp.float32))
+            logs.append(far_logs[away - 1, step])
         highest = functools.reduce(jnp.maximum, logs)
         weights = [jnp.exp(log - highest) for log in logs]
         total = functools.reduce(jnp.add, weights)
-        merged = spread(weights[0] / total) * pass_part[fars - 1, step].astype(jnp.float32)
-        for away in range(1, fars):
-            share = spread(weights[away] / total)
-            from_far[away, step].wait_recv()
-            merged = merged + share * far_part[away - 1, step].astype(jnp.float32)
+        merged = functools.reduce(
+            jnp.add, [spread(weight / total) * part for weight, part in zip(weights, parts)]
+        )
         columns = pl.ds(pl.multiple_of(level * HEAD_DIM, HEAD_DIM), HEAD_DIM)
         if step:
             done[step - 1] = merged.astype(jnp.bfloat16)
@@ -576,7 +567,7 @@
         return pltpu.VMEM(lead + (rows, HEAD_DIM), jnp.bfloat16)
 
     def logs_held(*lead):
-        return pltpu.VMEM(lead + (heads, 1, rows), jnp.float32)
+        return pltpu.VMEM(lead + (1, rows), jnp.float32)
 
     near_shape, far_shape = (nears - 1, fars * heads), (fars - 1, heads)
     return pl.pallas_call(
@@ -589,13 +580,13 @@
         out_specs=pl.BlockSpec(memory_space=pltpu.VMEM),
         scratch_shapes=[
             pltpu.VMEM((2 * rows, HEAD_DIM), jnp.float32),
-            held(shards), pltpu.VMEM((shards, 1, rows), jnp.float32),
-            held(*near_shape), logs_held(nears - 1, fars),
-            held(*far_shape), logs_held(fars - 1),
-            held(fars, heads), logs_held(fars),
+            held(shards), logs_held(shards),
+            held(*near_shape), logs_held(*near_shape),
+            held(*far_shape), logs_held(*far_shape),
+            held(*far_shape), logs_held(*far_shape),
             held(heads - 1),
-            dma(near_shape), dma(near_shape), dma((nears - 1, fars)), dma((nears - 1, fars)),
-            dma(far_shape), dma(far_shape), dma((fars - 1,)), dma((fars - 1,)),
+            dma(near_shape), dma(near_shape), dma(near_shape), dma(near_shape),
+            dma(far_shape), dma(far_shape), dma(far_shape), dma(far_shape),
             dma((heads - 1,)), dma((heads - 1,)),
         ],
         compiler_params=pltpu.CompilerParams(

time: 92.9 us -> 85.5 us (0.920)
  Pallas kernels: 88.7 us -> 81.2 us
    pallas_call x1, Pallas kernels: 32.4 us -> 25 us  [send_back(): pl.pallas_call(functools.partial(send_kernel, plan), out_shape=jax.ShapeD...]
where the time goes in v5:
time: 85.5 us; the launch traced here: 85.2 us
  Pallas kernels  81.2 us (95%)
  local copies, waits for them, and re-layouts  3.24 us (4%)
    pallas_call x1, Pallas kernels, bring_in(): pl.pallas_call(functools.partial(bring_kernel, plan), out_shape=(jax.Shap...  38 us
    pallas_call x1, Pallas kernels, send_back(): pl.pallas_call(functools.partial(send_kernel, plan), out_shape=jax.ShapeD...  25 us
    pallas_call x1, Pallas kernels, local_attend(): pl.pallas_call(local_kernel, out_shape=jax.ShapeDtypeStruct((2 * bound +...  18.2 us
    unnamed x5, local copies, waits for them, and re-layouts  3.24 us

profile of v5, /device:TPU:0, one launch (start us, length us, event | category | flops | bytes accessed | tf_op | source)
XLA Modules:
  0.0 85.2 jit_solution(2020901531659968796)
XLA Ops:
  0.0 0.7 multiply_add_fusion
  0.7 0.0 copy-start
  0.7 1.2 %copy-done = bf16[512,1024]{1,0:T(8,128)(2,1)S(1)} copy-done((bf16[512,1024]{1,0:T(8,128)(2,1)S(1)}, bf16[512,1024]{1,0:T(8,128)(2,1)}, u32[]{:S(2)}) %copy-start) | copy-done | bytes 1048600
  1.9 0.0 copy-start.1
  1.9 1.2 %copy-done.1 = bf16[512,1024]{1,0:T(8,128)(2,1)S(1)} copy-done((bf16[512,1024]{1,0:T(8,128)(2,1)S(1)}, bf16[512,1024]{1,0:T(8,128)(2,1)}, u32[]{:S(2)}) %copy-start.1) | copy-done | bytes 1048600
  3.2 38.0 %bring_in.1 = (bf16[16,2,512,128]{3,2,1,0:T(8,128)(2,1)S(1)}, s32[16,4,128]{2,1,0:T(4,128)S(1)}) custom-call(bf16[512,1024]{1,0:T(8,128)(2,1)S(1)} %copy-done, bf16[512,1024]{1,0:T(8,128)(2,1)S(1)} %copy-done.1, s32[4,128]{1,0:T(4,128)S(1)} %bitcast.2), custom_call_target="tpu_custom_call" | custom-call | tf_op jit(solution)/shard_map/bring_in/pallas_call | solution.py:397
  41.2 18.2 %local_attend.1.both_ref = f32[9224,128]{1,0:T(8,128)S(1)} custom-call(s32[64,128]{1,0:T(8,128)S(1)} %get-tuple-element.9.put_ref, bf16[16,2,512,128]{3,2,1,0:T(8,128)(2,1)S(1)} %get-tuple-element.8.tokens_ref), custom_call_target="tpu_custom_call" | custom-call | tf_op jit(solution)/shard_map/local_attend/pallas_call | solution.py:219
  59.4 25.0 %send_back.1 = bf16[512,512]{1,0:T(8,128)(2,1)S(1)} custom-call(s32[64,128]{1,0:T(8,128)S(1)} %get-tuple-element.10.take_ref, f32[9224,128]{1,0:T(8,128)S(1)} %local_attend.1.both_ref), custom_call_target="tpu_custom_call" | custom-call | tf_op jit(solution)/shard_map/send_back/pallas_call | solution.py:573
  84.4 0.8 copy.6
  (2 shorter events, 0.0 us)
Async XLA Ops:
  0.7 1.2 %copy-start = (bf16[512,1024]{1,0:T(8,128)(2,1)S(1)}, bf16[512,1024]{1,0:T(8,128)(2,1)}, u32[]{:S(2)}) copy-start(bf16[512,1024]{1,0:T(8,128)(2,1)} %qk_ref.1) | copy-start | bytes 3145732
  1.9 1.2 %copy-start.1 = (bf16[512,1024]{1,0:T(8,128)(2,1)S(1)}, bf16[512,1024]{1,0:T(8,128)(2,1)}, u32[]{:S(2)}) copy-start(bf16[512,1024]{1,0:T(8,128)(2,1)} %values_ref.1) | copy-start | bytes 3145732

commit v6 on v5

--- a/solution.py
+++ b/solution.py
@@ -293,7 +293,7 @@
     sent = []
     line = {}
     for k in range(2):
-        for step in near_first(heads):
+        for step in near_first(heads)[::-1]:
             to = lax.rem(level + step, heads)
             copy = remote(
                 fields[k].at[:, columns(to)], tokens_ref.at[mine, k],
@@ -352,7 +352,7 @@
             ).wait_recv()
             pass_near(source, k, turn * heads + step)
 
-    order = [(step, k) for k in range(2) for step in near_first(heads)]
+    order = [(step, k) for k in range(2) for step in near_first(heads)[::-1]]
     for k in range(2):
         own[k].wait()
         pass_far(mine, k, 0)

time: 85.5 us -> 86.5 us (1.012)
  Pallas kernels: 81.2 us -> 82.3 us
    pallas_call x1, Pallas kernels: 38 us -> 40.6 us  [bring_in(): pl.pallas_call(functools.partial(bring_kernel, plan), out_shape=(jax.Shap...]
    pallas_call x1, Pallas kernels: 25 us -> 23.4 us  [send_back(): pl.pallas_call(functools.partial(send_kernel, plan), out_shape=jax.ShapeD...]
where the time goes in v6:
time: 86.5 us; the launch traced here: 86.3 us
  Pallas kernels  82.3 us (95%)
  local copies, waits for them, and re-layouts  3.24 us (4%)
    pallas_call x1, Pallas kernels, bring_in(): pl.pallas_call(functools.partial(bring_kernel, plan), out_shape=(jax.Shap...  40.6 us
    pallas_call x1, Pallas kernels, send_back(): pl.pallas_call(functools.partial(send_kernel, plan), out_shape=jax.ShapeD...  23.4 us
    pallas_call x1, Pallas kernels, local_attend(): pl.pallas_call(local_kernel, out_shape=jax.ShapeDtypeStruct((2 * bound +...  18.2 us
    unnamed x5, local copies, waits for them, and re-layouts  3.24 us

profile of v6, /device:TPU:0, one launch (start us, length us, event | category | flops | bytes accessed | tf_op | source)
XLA Modules:
  0.0 86.3 jit_solution(13262627289046112837)
XLA Ops:
  0.0 0.7 multiply_add_fusion
  0.7 0.0 copy-start
  0.7 1.2 %copy-done = bf16[512,1024]{1,0:T(8,128)(2,1)S(1)} copy-done((bf16[512,1024]{1,0:T(8,128)(2,1)S(1)}, bf16[512,1024]{1,0:T(8,128)(2,1)}, u32[]{:S(2)}) %copy-start) | copy-done | bytes 1048600
  1.9 0.0 copy-start.1
  1.9 1.2 %copy-done.1 = bf16[512,1024]{1,0:T(8,128)(2,1)S(1)} copy-done((bf16[512,1024]{1,0:T(8,128)(2,1)S(1)}, bf16[512,1024]{1,0:T(8,128)(2,1)}, u32[]{:S(2)}) %copy-start.1) | copy-done | bytes 1048600
  3.2 40.6 %bring_in.1 = (bf16[16,2,512,128]{3,2,1,0:T(8,128)(2,1)S(1)}, s32[16,4,128]{2,1,0:T(4,128)S(1)}) custom-call(bf16[512,1024]{1,0:T(8,128)(2,1)S(1)} %copy-done, bf16[512,1024]{1,0:T(8,128)(2,1)S(1)} %copy-done.1, s32[4,128]{1,0:T(4,128)S(1)} %bitcast.2), custom_call_target="tpu_custom_call" | custom-call | tf_op jit(solution)/shard_map/bring_in/pallas_call | solution.py:397
  43.8 18.2 %local_attend.1.both_ref = f32[9224,128]{1,0:T(8,128)S(1)} custom-call(s32[64,128]{1,0:T(8,128)S(1)} %get-tuple-element.9.put_ref, bf16[16,2,512,128]{3,2,1,0:T(8,128)(2,1)S(1)} %get-tuple-element.8.tokens_ref), custom_call_target="tpu_custom_call" | custom-call | tf_op jit(solution)/shard_map/local_attend/pallas_call | solution.py:219
  62.1 23.4 %send_back.1 = bf16[512,512]{1,0:T(8,128)(2,1)S(1)} custom-call(s32[64,128]{1,0:T(8,128)S(1)} %get-tuple-element.10.take_ref, f32[9224,128]{1,0:T(8,128)S(1)} %local_attend.1.both_ref), custom_call_target="tpu_custom_call" | custom-call | tf_op jit(solution)/shard_map/send_back/pallas_call | solution.py:573
  85.5 0.8 copy.6
  (2 shorter events, 0.0 us)
Async XLA Ops:
  0.7 1.2 %copy-start = (bf16[512,1024]{1,0:T(8,128)(2,1)S(1)}, bf16[512,1024]{1,0:T(8,128)(2,1)}, u32[]{:S(2)}) copy-start(bf16[512,1024]{1,0:T(8,128)(2,1)} %qk_ref.1) | copy-start | bytes 3145732
  1.9 1.2 %copy-start.1 = (bf16[512,1024]{1,0:T(8,128)(2,1)S(1)}, bf16[512,1024]{1,0:T(8,128)(2,1)}, u32[]{:S(2)}) copy-start(bf16[512,1024]{1,0:T(8,128)(2,1)} %values_ref.1) | copy-start | bytes 3145732
